TPU v7x, 1024 devices: a whole 4x4x32 slice. The times are simulated.
1024 devices in a mesh: out: 32 (over z), con: 16 (over y, x_hi, core), occ: 2 (over x_lo).
Axes of the slice: x: 4 (x_hi: 2, x_lo: 2; x = x_hi * 2 + x_lo), y: 4, z: 32, core: 2. Of those that a mesh axis runs over, the one named last changes fastest.
Arguments:
- amplitudes: float32 [2048, 64, 64], P('con', 'occ', 'out'), may hold values from -6 to 6
- fit_out: float32 [1024, 8192], P('con', 'out'), may hold values from -0.12 to 0.12
- fit_con: float32 [1024, 2048], P(None, 'con'), may hold values from -0.12 to 0.12
- hole_hole: float32 [64, 64], replicated, may hold values from -0.75 to 0.75
Outputs:
- ladder: float32 [8192, 64, 64], P(('out', 'con'), 'occ')
All inputs are finite; a program needn't handle non-finite values.
Results may differ from a plain program's by a relative error of at most 0.000075.
Values sent between devices are 32-bit elements; how exact they have to be, the bound alone decides.
No kernel may reach another device: no remote copies, remote signals or barrier semaphores. Data moves between devices by JAX's collectives and lax.ppermute only.
A program may use at most 32 MiB of HBM per device.

v0:
```python
import jax
import jax.numpy as jnp
from jax import lax
from jax.sharding import PartitionSpec as P

highest = lax.Precision.HIGHEST


def copy_for_each(array, axis):
    length = lax.axis_size(axis)
    return lax.all_to_all(
        jnp.broadcast_to(array[None], (length, *array.shape)), axis, 0, 0, tiled=True
    )


def in_order(blocks, dim):
    blocks = jnp.moveaxis(blocks, 0, dim)
    lengths = blocks.shape
    return blocks.reshape(*lengths[:dim], lengths[dim] * lengths[dim + 1], *lengths[dim + 2 :])


def gather_directly(array, axis, dim):
    blocks = copy_for_each(array, axis)
    return in_order(blocks, dim)


def cut_along(array, dim, length):
    lengths = array.shape
    blocks = array.reshape(*lengths[:dim], length, lengths[dim] // length, *lengths[dim + 1 :])
    return jnp.moveaxis(blocks, dim, 0)


def summed_on_arrival(array, axis, dim):
    length = lax.axis_size(axis)
    blocks = lax.all_to_all(cut_along(array, dim, length), axis, 0, 0, tiled=True)
    return jnp.sum(blocks, axis=0)


def local(amplitudes, fit_out, fit_con, hole_hole):
    norbs = hole_hole.shape[0]
    dress = jnp.eye(norbs, dtype=jnp.float32) - hole_hole
    tile = jnp.dot(gather_directly(fit_out, "con", 0).T, fit_con, precision=highest)
    whole = gather_directly(amplitudes, "out", 2)
    kept_rows = tile.shape[0] // lax.axis_size("con")
    flat = whole.reshape(whole.shape[0], -1)
    product = jnp.dot(tile, flat, precision=highest)
    summed = summed_on_arrival(
        product.reshape(kept_rows * lax.axis_size("con"), whole.shape[1], whole.shape[2]), "con", 0
    )
    right = jnp.einsum("qim,jm->qij", summed, dress, precision=highest)
    complete = gather_directly(right, "occ", 1)
    own = summed.shape[1]
    first = lax.axis_index("occ") * own
    rows_dress = lax.dynamic_slice_in_dim(dress, first, own, 0)
    ladder = jnp.einsum("im,pmj->pij", rows_dress, complete, precision=highest)
    return ladder


def solution(mesh):
    placed = (P("con", "occ", "out"), P("con", "out"), P(None, "con"), P())
    return jax.shard_map(
        local, mesh=mesh, in_specs=placed, out_specs=P(("out", "con"), "occ", None), check_vma=False
    )
```

profile of v0, /device:TPU:1, one launch (start us, length us, event | category | flops | bytes accessed | tf_op | source)
XLA Modules:
  0.0 236.0 jit_solution(14945348141041958278)
XLA Ops:
  0.0 0.0 copy-start
  0.0 1.0 broadcast_in_dim.6
  1.0 33.4 %all_to_all.20 = f32[16,64,256]{2,1,0:T(8,128)S(1)} all-to-all(f32[16,64,256]{2,1,0:T(8,128)S(1)} %broadcast_in_dim.6), channel_id=1, replica_groups=mesh['out'=32,'con'=16,'occ'=2] {'con'}, dimensions={0} | all-to-all | bytes 2097152 | tf_op jit(solution)/shard_map/all_to_all | solution.py:11
  34.4 2.2 broadcast_in_dim.7
  36.7 20.0 %all-to-all-start.1 = ((f32[32,128,32,2]{1,3,2,0:T(2,128)}), f32[32,128,32,2]{1,3,2,0:T(2,128)S(1)}, u32[]{:S(2)}, u32[]{:S(2)}) async-start(f32[32,128,32,2]{1,3,2,0:T(2,128)} %broadcast_in_dim.7), calls=%async_computation.1 | async-start | bytes 2097152 | tf_op jit(solution)/shard_map/all_to_all | solution.py:11
  56.7 1.4 copy.8
  58.1 0.0 copy-done
  58.1 2.2 convolution_bitcast_fusion.1
  60.3 101.8 %all-to-all-done.1 = f32[32,128,32,2]{1,3,2,0:T(2,128)S(1)} async-done(((f32[32,128,32,2]{1,3,2,0:T(2,128)}), f32[32,128,32,2]{1,3,2,0:T(2,128)S(1)}, u32[]{:S(2)}, u32[]{:S(2)}) %all-to-all-start.1) | async-done | bytes 1048608 | tf_op jit(solution)/shard_map/all_to_all | solution.py:11
  162.0 0.6 copy.9
  162.6 5.0 %convolution_bitcast_fusion.2 = f32[16,32,16,64]{3,2,1,0:T(8,128)} fusion(f32[16,16,128,1]{2,1,3,0:T(8,128)S(1)} %convolution_bitcast_fusion.1, f32[32,64,128,1]{2,1,0,3:T(8,128)S(1)} %bitcast.40), kind=kOutput, calls=%fused_computation.12 | convolution fusion | flops 805306368 | bytes 3276800 | tf_op jit(solution)/shard_map/dot_general | solution.py:46
  167.6 5.5 %reshape.19 = f32[16,1,32768]{2,1,0:T(1,128)} reshape(f32[16,32,16,64]{3,2,1,0:T(8,128)} %convolution_bitcast_fusion.2) | data formatting | bytes 4194304
  173.1 8.0 %all-to-all-start.2 = ((f32[16,1,32768]{2,1,0:T(1,128)}), f32[16,1,32768]{2,1,0:T(1,128)S(1)}, u32[]{:S(2)}, u32[]{:S(2)}) async-start(f32[16,1,32768]{2,1,0:T(1,128)} %reshape.19), calls=%async_computation.2 | async-start | bytes 4194304 | tf_op jit(solution)/shard_map/all_to_all | solution.py:35
  181.1 28.3 %all-to-all-done.2 = f32[16,1,32768]{2,1,0:T(1,128)S(1)} async-done(((f32[16,1,32768]{2,1,0:T(1,128)}), f32[16,1,32768]{2,1,0:T(1,128)S(1)}, u32[]{:S(2)}, u32[]{:S(2)}) %all-to-all-start.2) | async-done | bytes 2097184 | tf_op jit(solution)/shard_map/all_to_all | solution.py:35
  209.4 0.0 copy-start.1
  209.5 1.3 copy-done.1
  210.8 0.5 broadcast.3
  211.3 7.2 %reduce = f32[16,32768]{1,0:T(8,128)S(1)} reduce(f32[16,1,32768]{2,1,0:T(1,128)} %copy-done.1, f32[]{:T(128)} %broadcast.3), dimensions={1}, to_apply=%all_to_all.14.reduce_sub_computation | reduce | bytes 4194308 | tf_op jit(solution)/shard_map/all_to_all | solution.py:35
  218.6 0.0 copy-start.2
  218.6 3.0 %reshape.20 = f32[16,32,16,64]{3,2,1,0:T(8,128)} reshape(f32[16,32768]{1,0:T(8,128)S(1)} %reduce) | data formatting | bytes 4194304
  221.6 2.5 %bitcast_reduce_fusion = f32[16,32,64]{2,0,1:T(8,128)S(1)} fusion(f32[16,32,16,64]{3,2,1,0:T(8,128)} %reshape.20), kind=kLoop, calls=%fused_computation.11 | loop fusion | flops 491520 | bytes 2228224 | tf_op jit(solution)/shard_map/reduce_sum | solution.py:36
  224.1 0.0 copy-done.2
  224.1 0.4 fusion.1
  224.5 0.1 broadcast_in_dim.8
  224.6 1.0 reshape.21
  225.6 3.4 %all-to-all-start.3 = ((f32[2,1,32768]{2,1,0:T(1,128)}), f32[2,1,32768]{2,1,0:T(1,128)S(1)}, u32[]{:S(2)}, u32[]{:S(2)}) async-start(f32[2,1,32768]{2,1,0:T(1,128)} %reshape.21), calls=%async_computation.3 | async-start | bytes 524288 | tf_op jit(solution)/shard_map/all_to_all | solution.py:11
  229.1 4.0 %all-to-all-done.3 = f32[2,1,32768]{2,1,0:T(1,128)S(1)} async-done(((f32[2,1,32768]{2,1,0:T(1,128)}), f32[2,1,32768]{2,1,0:T(1,128)S(1)}, u32[]{:S(2)}, u32[]{:S(2)}) %all-to-all-start.3) | async-done | bytes 262176 | tf_op jit(solution)/shard_map/all_to_all | solution.py:11
  233.1 1.4 reduce.1
  234.5 0.3 reshape.22
  234.9 1.1 convolution_bitcast_fusion
  (2 shorter events, 0.0 us)
Async XLA Ops:
  0.0 58.1 %copy-start = (f32[1024,128]{1,0:T(8,128)S(1)}, f32[1024,128]{1,0:T(8,128)}, u32[]{:S(2)}) copy-start(f32[1024,128]{1,0:T(8,128)} %param.6) | copy-start | bytes 1572868
  36.7 125.4 %all-to-all-start.1 = ((f32[32,128,32,2]{1,3,2,0:T(2,128)}), f32[32,128,32,2]{1,3,2,0:T(2,128)S(1)}, u32[]{:S(2)}, u32[]{:S(2)}) async-start(f32[32,128,32,2]{1,3,2,0:T(2,128)} %broadcast_in_dim.7), calls=%async_computation.1 | async-start | bytes 2097152 | tf_op jit(solution)/shard_map/all_to_all | solution.py:11
  173.1 36.3 %all-to-all-start.2 = ((f32[16,1,32768]{2,1,0:T(1,128)}), f32[16,1,32768]{2,1,0:T(1,128)S(1)}, u32[]{:S(2)}, u32[]{:S(2)}) async-start(f32[16,1,32768]{2,1,0:T(1,128)} %reshape.19), calls=%async_computation.2 | async-start | bytes 4194304 | tf_op jit(solution)/shard_map/all_to_all | solution.py:35
  209.4 1.3 copy-start.1
  218.6 5.5 %copy-start.2 = (f32[64,64]{1,0:T(8,128)S(1)}, f32[64,64]{1,0:T(8,128)}, u32[]{:S(2)}) copy-start(f32[64,64]{1,0:T(8,128)} %param.7) | copy-start | bytes 49156
  225.6 7.5 %all-to-all-start.3 = ((f32[2,1,32768]{2,1,0:T(1,128)}), f32[2,1,32768]{2,1,0:T(1,128)S(1)}, u32[]{:S(2)}, u32[]{:S(2)}) async-start(f32[2,1,32768]{2,1,0:T(1,128)} %reshape.21), calls=%async_computation.3 | async-start | bytes 524288 | tf_op jit(solution)/shard_map/all_to_all | solution.py:11
where the time goes:
time: 237 us; the launch traced here: 236 us
  waiting for transfers between devices  134 us (57%)
  blocking collectives  33.4 us (14%)
  starting transfers between devices  31.5 us (13%)
  local copies, waits for them, and re-layouts  17 us (7%)
  other arithmetic  11.2 us (5%)
  matrix products  8.74 us (4%)
    all_to_all x2, waiting for transfers between devices, copy_for_each(): lax.all_to_all(jnp.broadcast_to(array[None], (length, *array.shape)), axi...  106 us
    all_to_all x1, blocking collectives, copy_for_each(): lax.all_to_all(jnp.broadcast_to(array[None], (length, *array.shape)), axi...  33.4 us
    all_to_all x1, waiting for transfers between devices, summed_on_arrival(): lax.all_to_all(cut_along(array, dim, length), axis, 0, 0, tiled=True)  28.3 us
    all_to_all x2, starting transfers between devices, copy_for_each(): lax.all_to_all(jnp.broadcast_to(array[None], (length, *array.shape)), axi...  23.5 us
    unnamed x10, local copies, waits for them, and re-layouts  11.2 us
    all_to_all x1, starting transfers between devices, summed_on_arrival(): lax.all_to_all(cut_along(array, dim, length), axis, 0, 0, tiled=True)  8 us
    all_to_all x1, other arithmetic, summed_on_arrival(): lax.all_to_all(cut_along(array, dim, length), axis, 0, 0, tiled=True)  7.25 us
    dot_general x1, matrix products, local(): product = jnp.dot(tile, flat, precision=highest)  5 us
  transfers between devices with their start and end apart: 3, of which 3 were waited for; matrix products, arithmetic and copies ran while one was open for 2% of the time, Pallas kernels for 0%

commit v1 on v0

v1 whole, which is shorter than its diff:
```python
import jax
import jax.numpy as jnp
from jax import lax
from jax.sharding import PartitionSpec as P

highest = lax.Precision.HIGHEST


def copy_for_each(array, axis, groups=None):
    length = lax.axis_size(axis) if groups is None else len(groups[0])
    return lax.all_to_all(
        jnp.broadcast_to(array[None], (length, *array.shape)),
        axis, 0, 0, tiled=True, axis_index_groups=groups,
    )


def local(amplitudes, fit_out, fit_con, hole_hole):
    norbs = hole_hole.shape[0]
    outs, cons, occs = lax.axis_size("out"), lax.axis_size("con"), lax.axis_size("occ")
    plane = cons * occs
    naux = fit_con.shape[0]
    own = amplitudes.shape[1]
    cols = amplitudes.shape[2]
    kept = norbs // plane
    dress = jnp.eye(norbs, dtype=jnp.float32) - hole_hole

    first = lax.axis_index("occ") * own
    columns = lax.dynamic_slice_in_dim(dress, first, own, 1)
    half = jnp.einsum("im,qmj->ijq", columns, amplitudes, precision=highest)
    half = half.reshape(-1, half.shape[2])
    share = jnp.einsum("pq,lq->pl", half, fit_con, precision=highest)
    share = share.reshape(occs, cons, kept * cols, naux)
    share = jnp.swapaxes(share, 0, 1).reshape(plane, kept * cols, naux)
    parts = lax.all_to_all(share, ("con", "occ"), 0, 0, tiled=True)
    fitted = jnp.sum(parts, axis=0)
    parity = [[2 * k + r for k in range(outs // 2)] for r in range(2)]
    pairs = [[2 * k + r for r in range(2)] for k in range(outs // 2)]
    strided = lax.all_gather(fitted, "out", axis=0, axis_index_groups=parity)
    whole = copy_for_each(strided, "out", pairs)
    factors = copy_for_each(fit_out, "con")
    factors = factors.reshape(naux, -1)
    ladder = jnp.einsum("pl,la->pa", whole.reshape(kept * norbs, naux), factors, precision=highest)
    orders = dress.T.reshape(outs // 2, 2, cols, norbs)
    orders = jnp.swapaxes(orders, 0, 1)
    blocks = jnp.einsum("ik,zhjn->zhkjin", jnp.eye(kept, dtype=jnp.float32), orders, precision=highest)
    blocks = blocks.reshape(kept * norbs, kept * norbs)
    ladder = jnp.einsum("pa,pn->an", ladder, blocks, precision=highest)
    rows = ladder.shape[0] // cons
    ladder = ladder.reshape(cons, rows, kept * norbs)
    ladder = lax.all_to_all(ladder, "con", 0, 0, tiled=True)
    ladder = ladder.reshape(cons, rows, kept, norbs)
    return jnp.swapaxes(ladder, 0, 1).reshape(rows, cons * kept, norbs)


def solution(mesh):
    placed = (P("con", "occ", "out"), P("con", "out"), P(None, "con"), P())
    return jax.shard_map(
        local, mesh=mesh, in_specs=placed, out_specs=P(("out", "con"), "occ", None), check_vma=False
    )
```

time: 237 us -> 116 us (0.49)
  waiting for transfers between devices: 134 us -> 16.6 us
  blocking collectives: 33.4 us -> 79.8 us
  starting transfers between devices: 31.5 us -> 12.8 us
  local copies, waits for them, and re-layouts: 17 us -> 4.64 us
  other arithmetic: 11.2 us -> 0.22 us
  matrix products: 8.74 us -> 1.73 us
    all_to_all x2 -> x1, waiting for transfers between devices: 106 us -> 16.6 us  [copy_for_each(): lax.all_to_all(jnp.broadcast_to(array[None], (length, *array.shape)), axi...]
    all_to_all x0 -> x2, blocking collectives: none -> 38.4 us  [the longest x1 27.3 us: local(): parts = lax.all_to_all(share, ('con', 'occ'), 0, 0, tiled=True)]
    all_gather x0 -> x1, blocking collectives: none -> 33.5 us  [local(): strided = lax.all_gather(fitted, 'out', axis=0, axis_index_groups=parity)]
    all_to_all x1 -> x0, waiting for transfers between devices: 28.3 us -> none  [summed_on_arrival(): lax.all_to_all(cut_along(array, dim, length), axis, 0, 0, tiled=True)]
    all_to_all x1, blocking collectives: 33.4 us -> 7.97 us  [copy_for_each(): lax.all_to_all(jnp.broadcast_to(array[None], (length, *array.shape)), axi...]
    all_to_all x2 -> x1, starting transfers between devices: 23.5 us -> 12.8 us  [copy_for_each(): lax.all_to_all(jnp.broadcast_to(array[None], (length, *array.shape)), axi...]
    unnamed x10 -> x7, local copies, waits for them, and re-layouts: 11.2 us -> 1.64 us
    all_to_all x2 -> x0, other arithmetic: 8.65 us -> none  [the longest x1 7.25 us: summed_on_arrival(): lax.all_to_all(cut_along(array, dim, length), axis, 0, 0, tiled=True)]
  transfers between devices with their start and end apart: 3 -> 1, of which waited for: 3 -> 1; matrix products, arithmetic and copies ran while one was open for 2% -> 0% of each run, Pallas kernels for 0% -> 0%
where the time goes in v1:
time: 116 us
  blocking collectives  79.8 us (69%)
  waiting for transfers between devices  16.6 us (14%)
  starting transfers between devices  12.8 us (11%)
  local copies, waits for them, and re-layouts  4.64 us (4%)
  matrix products  1.73 us (1%)
    all_gather x1, blocking collectives, local(): strided = lax.all_gather(fitted, 'out', axis=0, axis_index_groups=parity)  33.5 us
    all_to_all x1, blocking collectives, local(): parts = lax.all_to_all(share, ('con', 'occ'), 0, 0, tiled=True)  27.3 us
    all_to_all x1, waiting for transfers between devices, copy_for_each(): lax.all_to_all(jnp.broadcast_to(array[None], (length, *array.shape)), axi...  16.6 us
    all_to_all x1, starting transfers between devices, copy_for_each(): lax.all_to_all(jnp.broadcast_to(array[None], (length, *array.shape)), axi...  12.8 us
    all_to_all x1, blocking collectives, local(): ladder = lax.all_to_all(ladder, 'con', 0, 0, tiled=True)  11.1 us
    all_to_all x1, blocking collectives, copy_for_each(): lax.all_to_all(jnp.broadcast_to(array[None], (length, *array.shape)), axi...  7.97 us
  transfers between devices with their start and end apart: 1, of which 1 were waited for; matrix products, arithmetic and copies ran while one was open for 0% of the time, Pallas kernels for 0%

profile of v1, /device:TPU:1, one launch (start us, length us, event | category | flops | bytes accessed | tf_op | source)
XLA Modules:
  0.0 115.9 jit_solution(4383137159335416309)
XLA Ops:
  0.0 0.0 copy-start
  0.0 0.9 copy.18
  0.9 0.0 copy-start.2
  0.9 0.7 copy-done.2
  1.7 0.3 convolution_bitcast_fusion.2
  1.9 0.1 copy.20
  2.0 0.0 copy-done
  2.0 0.6 convolution_bitcast_fusion
  2.6 0.3 copy.22
  2.9 27.3 %all_to_all.20 = f32[32,4,1024]{2,1,0:T(4,128)S(1)} all-to-all(f32[32,4,1024]{2,1,0:T(4,128)S(1)} %bitcast.33), channel_id=1, replica_groups=mesh['out'=32,'con'=16,'occ'=2] {'con','occ'}, dimensions={0} | all-to-all | bytes 1048576 | tf_op jit(solution)/shard_map/all_to_all | solution.py:34
  30.2 0.1 reduce_sum.9
  30.3 33.5 %all-gather.1 = f32[16,4,1024]{2,1,0:T(4,128)S(1)} all-gather(f32[1,4,1024]{2,1,0:T(4,128)S(1)} %bitcast.38), channel_id=2, replica_groups={{0,64,128,192,256,320,384,448,512,576,640,704,768,832,896,960},{32,96,1..., dimensions={0}, use_global_device_ids=true | all-gather | bytes 278528 | tf_op jit(solution)/shard_map/all_gather | solution.py:38
  63.8 0.1 broadcast_in_dim.4
  63.9 0.0 copy-start.1
  63.9 8.0 %all_to_all.21 = f32[2,16,4,1024]{3,2,1,0:T(4,128)S(1)} all-to-all(f32[2,16,4,1024]{3,2,1,0:T(4,128)S(1)} %broadcast_in_dim.4), channel_id=1, replica_groups={{0,32},{64,96},{128,160},{192,224},{256,288},{320,352},{384,416},{448,4..., dimensions={0} | all-to-all | bytes 1048576 | tf_op jit(solution)/shard_map/all_to_all | solution.py:11
  71.9 0.0 copy-done.1
  71.9 1.1 broadcast_in_dim.5
  72.9 12.8 %all-to-all-start.2 = ((f32[16,64,256]{2,1,0:T(8,128)}), f32[16,64,256]{2,1,0:T(8,128)S(1)}, u32[]{:S(2)}, u32[]{:S(2)}) async-start(f32[16,64,256]{2,1,0:T(8,128)} %broadcast_in_dim.5), calls=%async_computation.2 | async-start | bytes 2097152 | tf_op jit(solution)/shard_map/all_to_all | solution.py:11
  85.7 0.1 multiply_bitcast_fusion
  85.8 0.1 reshape.42
  85.9 0.2 reshape.30
  86.1 16.6 %all-to-all-done.2 = f32[16,64,256]{2,1,0:T(8,128)S(1)} async-done(((f32[16,64,256]{2,1,0:T(8,128)}), f32[16,64,256]{2,1,0:T(8,128)S(1)}, u32[]{:S(2)}, u32[]{:S(2)}) %all-to-all-start.2) | async-done | bytes 1048608 | tf_op jit(solution)/shard_map/all_to_all | solution.py:11
  102.8 0.6 convolution_bitcast_fusion.1
  103.4 0.1 copy.23
  103.5 0.3 fusion.6
  103.8 11.1 %all_to_all.22 = f32[16,16,128]{2,1,0:T(8,128)S(1)} all-to-all(f32[16,16,128]{2,1,0:T(8,128)S(1)} %fusion.6), channel_id=1, replica_groups=mesh['out'=32,'con'=16,'occ'=2] {'con'}, dimensions={0} | all-to-all | bytes 262144 | tf_op jit(solution)/shard_map/all_to_all | solution.py:50
  114.9 0.2 reshape.34
  115.1 0.8 copy.25
  (2 shorter events, 0.0 us)
Async XLA Ops:
  0.0 2.0 %copy-start = (f32[1024,128]{1,0:T(8,128)S(1)}, f32[1024,128]{1,0:T(8,128)}, u32[]{:S(2)}) copy-start(f32[1024,128]{1,0:T(8,128)} %param.6) | copy-start | bytes 1572868
  0.9 0.8 copy-start.2
  63.9 8.0 %copy-start.1 = (f32[64,256]{1,0:T(8,128)S(1)}, f32[64,256]{1,0:T(8,128)}, u32[]{:S(2)}) copy-start(f32[64,256]{1,0:T(8,128)} %param.5) | copy-start | bytes 196612
  72.9 29.8 %all-to-all-start.2 = ((f32[16,64,256]{2,1,0:T(8,128)}), f32[16,64,256]{2,1,0:T(8,128)S(1)}, u32[]{:S(2)}, u32[]{:S(2)}) async-start(f32[16,64,256]{2,1,0:T(8,128)} %broadcast_in_dim.5), calls=%async_computation.2 | async-start | bytes 2097152 | tf_op jit(solution)/shard_map/all_to_all | solution.py:11

commit v2 on v1

v2 whole, which is shorter than its diff:
```python
import jax
import jax.numpy as jnp
from jax import lax
from jax.experimental import pallas as pl
from jax.experimental.pallas import tpu as pltpu
from jax.sharding import Mesh, PartitionSpec as P

highest = lax.Precision.HIGHEST
plane = ("con", "occ")
pair = ("out_lo", "con")
lanes = 128
room = 16 * 1024 * 1024


def dot(a, b):
    return jnp.dot(a, b, precision=highest, preferred_element_type=jnp.float32)


def contract_kernel(fitted_ref, factors_ref, ladder_ref):
    total = dot(fitted_ref[...], factors_ref[...])
    blocks, rows, _ = ladder_ref.shape
    turned = total.T.reshape(blocks, 2, rows, total.shape[0])
    ladder_ref[...] = jnp.concatenate([turned[:, 0], turned[:, 1]], axis=-1)


def contract(fitted, factors, blocks):
    cols, pairs = fitted.shape[0], factors.shape[1]
    return pl.pallas_call(
        contract_kernel,
        out_shape=jax.ShapeDtypeStruct((blocks, pairs // blocks // 2, 2 * cols), jnp.float32),
        in_specs=[pl.BlockSpec(memory_space=pltpu.VMEM)] * 2,
        out_specs=pl.BlockSpec(memory_space=pltpu.VMEM),
        compiler_params=pltpu.CompilerParams(vmem_limit_bytes=room),
    )(fitted, factors)


def finish_kernel(ladder_ref, blocks_ref, out_ref, held):
    lots = blocks_ref.shape[0]
    total = None
    for z in range(lots):
        term = dot(ladder_ref[z], blocks_ref[z])
        total = term if z == 0 else total + term
    halves, kept, norbs = 2, held.shape[0] // 2, out_ref.shape[2]
    rows, cons = out_ref.shape[0] // halves, out_ref.shape[1] // kept
    for s in range(halves * kept):
        held[s] = total[:, s * lanes : (s + 1) * lanes]
    for h in range(halves):
        for i in range(kept):
            for r in range(rows):
                line = held[h * kept + i, pl.ds(r, cons, stride=rows), :]
                out_ref[h * rows + r, pl.ds(i, cons, stride=kept), :] = line[:, :norbs]


def finish(ladder, blocks, shape, kept):
    return pl.pallas_call(
        finish_kernel,
        out_shape=jax.ShapeDtypeStruct(shape, jnp.float32),
        in_specs=[pl.BlockSpec(memory_space=pltpu.VMEM)] * 2,
        out_specs=pl.BlockSpec(memory_space=pltpu.VMEM),
        scratch_shapes=[pltpu.VMEM((2 * kept, ladder.shape[1], lanes), jnp.float32)],
        compiler_params=pltpu.CompilerParams(vmem_limit_bytes=room),
    )(ladder, blocks)


def local(amplitudes, fit_out, fit_con, hole_hole):
    norbs = hole_hole.shape[0]
    naux = fit_con.shape[0]
    halves, lots = lax.axis_size("out_hi"), lax.axis_size("out_lo")
    cons, occs = lax.axis_size("con"), lax.axis_size("occ")
    own, cols = amplitudes.shape[1], amplitudes.shape[2]
    kept = norbs // (cons * occs)
    side = lax.axis_index("out_lo")
    dress = jnp.eye(norbs, dtype=jnp.float32) - hole_hole

    first = lax.axis_index("occ") * own
    columns = lax.dynamic_slice_in_dim(dress, first, own, 1)
    columns = jnp.swapaxes(columns.reshape(occs, cons, kept, own), 0, 1).reshape(norbs, own)
    half = jnp.einsum("im,qmj->ijq", columns, amplitudes, precision=highest)
    half = half.reshape(norbs * cols, half.shape[2])
    share = jnp.einsum("pq,lq->pl", half, fit_con, precision=highest)
    share = share.reshape(cons * occs, kept * cols, naux)
    parts = lax.all_to_all(share, plane, 0, 0, tiled=True)
    fitted = jnp.sum(parts, axis=0)
    whole = lax.all_gather(fitted, "out_hi", axis=0)
    whole = whole.reshape(halves * kept * cols, naux)
    other = lax.ppermute(fit_out, "out_lo", [(0, 1), (1, 0)])
    factors = jnp.concatenate(
        [jnp.where(side == 0, fit_out, other), jnp.where(side == 0, other, fit_out)], axis=1
    )
    factors = jnp.broadcast_to(factors[None], (cons, *factors.shape))
    factors = lax.all_to_all(factors, "con", 0, 0, tiled=True)
    factors = factors.reshape(naux, lots * fit_out.shape[1])
    ladder = contract(whole, factors, lots * cons)
    ladder = lax.all_to_all(ladder, pair, 0, 0, tiled=True)
    rows = fit_out.shape[1] // cons
    ladder = ladder.reshape(lots, cons * rows // 2, lanes)
    orders = jnp.swapaxes(dress.T.reshape(halves, lots, cols, norbs), 0, 1)
    orders = jnp.pad(orders, ((0, 0), (0, 0), (0, 0), (0, lanes - norbs)))
    orders = orders.reshape(lots, 1, halves, 1, cols, 1, 1, lanes)
    same = jnp.eye(2, dtype=jnp.float32).reshape(1, 2, 1, 1, 1, 2, 1, 1)
    kind = jnp.eye(kept, dtype=jnp.float32).reshape(1, 1, 1, kept, 1, 1, kept, 1)
    blocks = (orders * same * kind).reshape(lots, lanes, 2 * kept * lanes)
    return finish(ladder, blocks, (rows, cons * kept, norbs), kept)


def solution(mesh):
    lots = 2
    shape = dict(mesh.shape)
    devices = mesh.devices.reshape(shape["out"] // lots, lots, shape["con"], shape["occ"])
    finer = Mesh(devices, ("out_hi", "out_lo", "con", "occ"))
    out = ("out_hi", "out_lo")
    return jax.shard_map(
        local,
        mesh=finer,
        in_specs=(P("con", "occ", out), P("con", out), P(None, "con"), P()),
        out_specs=P((*out, "con"), "occ", None),
        check_vma=False,
    )
```

time: 116 us -> 98.3 us (0.85)
  blocking collectives: 79.8 us -> 33.4 us
  starting transfers between devices: 12.8 us -> 38.5 us
  Pallas kernels: 0 us -> 3.44 us
    all_to_all x3 -> x0, blocking collectives: 46.4 us -> none  [the longest x1 27.3 us: local(): parts = lax.all_to_all(share, ('con', 'occ'), 0, 0, tiled=True)]
    all_to_all x1 -> x3, starting transfers between devices: 12.8 us -> 36.5 us  [the longest x1 17.7 us: local(): parts = lax.all_to_all(share, plane, 0, 0, tiled=True)]
    all_to_all x1 -> x3, waiting for transfers between devices: 16.6 us -> 12.3 us  [the longest x1 7.15 us: local(): ladder = lax.all_to_all(ladder, pair, 0, 0, tiled=True)]
    pallas_call x0 -> x2, Pallas kernels: none -> 3.44 us  [the longest x1 2.13 us: contract(): pl.pallas_call(contract_kernel, out_shape=jax.ShapeDtypeStruct((blocks, p...]
    ppermute x0 -> x1, waiting for transfers between devices: none -> 3.37 us  [local(): other = lax.ppermute(fit_out, 'out_lo', [(0, 1), (1, 0)])]
    ppermute x0 -> x1, starting transfers between devices: none -> 1.92 us  [local(): other = lax.ppermute(fit_out, 'out_lo', [(0, 1), (1, 0)])]
    unnamed x7 -> x6, local copies, waits for them, and re-layouts: 1.64 us -> 0.12 us
  transfers between devices with their start and end apart: 1 -> 4, of which waited for: 1 -> 3; matrix products, arithmetic and copies ran while one was open for 0% -> 1% of each run, Pallas kernels for 0% -> 0%
where the time goes in v2:
time: 98.3 us; the launch traced here: 97.8 us
  starting transfers between devices  38.5 us (39%)
  blocking collectives  33.4 us (34%)
  waiting for transfers between devices  15.7 us (16%)
  local copies, waits for them, and re-layouts  4 us (4%)
  Pallas kernels  3.44 us (3%)
  matrix products  1.54 us (2%)
  other arithmetic  1.12 us (1%)
    all_gather x1, blocking collectives, local(): whole = lax.all_gather(fitted, 'out_hi', axis=0)  33.4 us
    all_to_all x1, starting transfers between devices, local(): parts = lax.all_to_all(share, plane, 0, 0, tiled=True)  17.7 us
    all_to_all x1, starting transfers between devices, local(): ladder = lax.all_to_all(ladder, pair, 0, 0, tiled=True)  13.7 us
    all_to_all x1, waiting for transfers between devices, local(): ladder = lax.all_to_all(ladder, pair, 0, 0, tiled=True)  7.15 us
    all_to_all x1, starting transfers between devices, local(): factors = lax.all_to_all(factors, 'con', 0, 0, tiled=True)  5.22 us
    all_to_all x1, waiting for transfers between devices, local(): parts = lax.all_to_all(share, plane, 0, 0, tiled=True)  5.13 us
    ppermute x1, waiting for transfers between devices, local(): other = lax.ppermute(fit_out, 'out_lo', [(0, 1), (1, 0)])  3.37 us
    pallas_call x1, Pallas kernels, contract(): pl.pallas_call(contract_kernel, out_shape=jax.ShapeDtypeStruct((blocks, p...  2.13 us
  transfers between devices with their start and end apart: 4, of which 3 were waited for; matrix products, arithmetic and copies ran while one was open for 1% of the time, Pallas kernels for 0%

profile of v2, /device:TPU:1, one launch (start us, length us, event | category | flops | bytes accessed | tf_op | source)
XLA Modules:
  0.0 97.8 jit_solution(5316855576320852068)
XLA Ops:
  0.0 0.0 copy-start
  0.0 0.0 copy-start.1
  0.0 0.8 fusion.4
  0.8 0.1 constant_dynamic-slice_fusion
  0.9 0.9 convolution_bitcast_fusion
  1.9 0.1 copy.17
  2.0 0.0 copy-done
  2.0 0.6 fusion
  2.6 1.1 %copy.19 = f32[32,4,1024]{2,1,0:T(4,128)} copy(f32[32,4,1024]{2,0,1:T(8,128)S(1)} %fusion) | data formatting | bytes 1048576 | tf_op jit(solution)/shard_map/pq,lq->pl/dot_general | solution.py:80
  3.7 17.7 %all-to-all-start = ((f32[32,4,1024]{2,1,0:T(4,128)}), f32[32,4,1024]{2,1,0:T(4,128)S(1)}, u32[]{:S(2)}, u32[]{:S(2)}) async-start(f32[32,4,1024]{2,1,0:T(4,128)} %copy.19), calls=%async_computation | async-start | bytes 1048576 | tf_op jit(solution)/shard_map/all_to_all | solution.py:82
  21.4 0.0 copy-done.1
  21.4 1.9 %collective-permute-start = (f32[64,256]{1,0:T(8,128)S(1)}, f32[64,256]{1,0:T(8,128)S(1)}, u32[]{:S(2)}, u32[]{:S(2)}) collective-permute-start(f32[64,256]{1,0:T(8,128)S(1)} %copy-done.1), channel_id=1, source_target_pairs={{0,32},{32,0},{1,33},{33,1},{2,34},{34,2},{3,35},{35,3},{4,36},{36... | collective-permute-start | bytes 196616 | tf_op jit(solution)/shard_map/ppermute | solution.py:86
  23.3 3.4 %collective-permute-done = f32[64,256]{1,0:T(8,128)S(1)} collective-permute-done((f32[64,256]{1,0:T(8,128)S(1)}, f32[64,256]{1,0:T(8,128)S(1)}, u32[]{:S(2)}, u32[]{:S(2)}) %collective-permute-start) | collective-permute-done | bytes 65568 | tf_op jit(solution)/shard_map/ppermute | solution.py:86
  26.7 5.1 %all-to-all-done = f32[32,4,1024]{2,1,0:T(4,128)S(1)} async-done(((f32[32,4,1024]{2,1,0:T(4,128)}), f32[32,4,1024]{2,1,0:T(4,128)S(1)}, u32[]{:S(2)}, u32[]{:S(2)}) %all-to-all-start) | async-done | bytes 524320 | tf_op jit(solution)/shard_map/all_to_all | solution.py:82
  31.9 1.6 %broadcast_in_dim.2 = f32[16,64,512]{2,1,0:T(8,128)} broadcast(f32[64,512]{1,0:T(8,128)S(1)} %pad_maximum_fusion), dimensions={1,2} | broadcast | bytes 2228224 | tf_op jit(solution)/shard_map/broadcast_in_dim | solution.py:90
  33.5 5.2 %all-to-all-start.1 = ((f32[16,64,512]{2,1,0:T(8,128)}), f32[16,64,512]{2,1,0:T(8,128)S(1)}, u32[]{:S(2)}, u32[]{:S(2)}) async-start(f32[16,64,512]{2,1,0:T(8,128)} %broadcast_in_dim.2), calls=%async_computation.1 | async-start | bytes 4194304 | tf_op jit(solution)/shard_map/all_to_all | solution.py:91
  38.7 0.1 reduce_sum.9
  38.8 33.4 %all-gather.1 = f32[16,4,1024]{2,1,0:T(4,128)S(1)} all-gather(f32[1,4,1024]{2,1,0:T(4,128)S(1)} %bitcast.27), channel_id=2, replica_groups=mesh['out_hi'=16,'out_lo'=2,'con'=16,'occ'=2] {'out_hi'}, dimensions={0}, use_global_device_ids=true | all-gather | bytes 278528 | tf_op jit(solution)/shard_map/all_gather | solution.py:84
  72.2 0.1 reshape.61.fitted_ref
  72.3 0.0 all-to-all-done.1
  72.3 2.1 %shard_map.46 = f32[32,8,128]{2,1,0:T(8,128)} custom-call(f32[64,1024]{1,0:T(8,128)S(1)} %reshape.61.fitted_ref, f32[1024,512]{1,0:T(8,128)S(1)} %bitcast.21), custom_call_target="tpu_custom_call" | custom-call | tf_op jit(solution)/shard_map/pallas_call | solution.py:28
  74.5 13.7 %all-to-all-start.2 = ((f32[32,8,128]{2,1,0:T(8,128)}), f32[32,8,128]{2,1,0:T(8,128)S(1)}, u32[]{:S(2)}, u32[]{:S(2)}) async-start(f32[32,8,128]{2,1,0:T(8,128)} %shard_map.46), calls=%async_computation.2 | async-start | bytes 262144 | tf_op jit(solution)/shard_map/all_to_all | solution.py:94
  88.1 0.1 copy.20
  88.3 0.1 broadcast_multiply_fusion.1
  88.4 0.1 mul.45
  88.5 0.4 mul.46
  88.9 0.1 mul.47
  89.1 0.2 mul.48
  89.3 0.1 broadcast_multiply_fusion.blocks_ref
  89.4 7.2 %all-to-all-done.2 = f32[32,8,128]{2,1,0:T(8,128)S(1)} async-done(((f32[32,8,128]{2,1,0:T(8,128)}), f32[32,8,128]{2,1,0:T(8,128)S(1)}, u32[]{:S(2)}, u32[]{:S(2)}) %all-to-all-start.2) | async-done | bytes 131104 | tf_op jit(solution)/shard_map/all_to_all | solution.py:94
  96.5 1.3 %shard_map.47 = f32[16,32,64]{2,1,0:T(8,128)} custom-call(f32[2,128,128]{2,1,0:T(8,128)S(1)} %bitcast.22, f32[2,128,512]{2,1,0:T(8,128)S(1)} %broadcast_multiply_fusion.blocks_ref), custom_call_target="tpu_custom_call" | custom-call | tf_op jit(solution)/shard_map/pallas_call | solution.py:55
  (6 shorter events, 0.1 us)
Async XLA Ops:
  0.0 2.0 %copy-start = (f32[1024,128]{1,0:T(8,128)S(1)}, f32[1024,128]{1,0:T(8,128)}, u32[]{:S(2)}) copy-start(f32[1024,128]{1,0:T(8,128)} %param.6) | copy-start | bytes 1572868
  0.0 21.4 %copy-start.1 = (f32[64,256]{1,0:T(8,128)S(1)}, f32[64,256]{1,0:T(8,128)}, u32[]{:S(2)}) copy-start(f32[64,256]{1,0:T(8,128)} %param.5) | copy-start | bytes 196612
  3.7 28.2 %all-to-all-start = ((f32[32,4,1024]{2,1,0:T(4,128)}), f32[32,4,1024]{2,1,0:T(4,128)S(1)}, u32[]{:S(2)}, u32[]{:S(2)}) async-start(f32[32,4,1024]{2,1,0:T(4,128)} %copy.19), calls=%async_computation | async-start | bytes 1048576 | tf_op jit(solution)/shard_map/all_to_all | solution.py:82
  21.4 5.3 %collective-permute-start = (f32[64,256]{1,0:T(8,128)S(1)}, f32[64,256]{1,0:T(8,128)S(1)}, u32[]{:S(2)}, u32[]{:S(2)}) collective-permute-start(f32[64,256]{1,0:T(8,128)S(1)} %copy-done.1), channel_id=1, source_target_pairs={{0,32},{32,0},{1,33},{33,1},{2,34},{34,2},{3,35},{35,3},{4,36},{36... | collective-permute-start | bytes 196616 | tf_op jit(solution)/shard_map/ppermute | solution.py:86
  33.5 38.9 %all-to-all-start.1 = ((f32[16,64,512]{2,1,0:T(8,128)}), f32[16,64,512]{2,1,0:T(8,128)S(1)}, u32[]{:S(2)}, u32[]{:S(2)}) async-start(f32[16,64,512]{2,1,0:T(8,128)} %broadcast_in_dim.2), calls=%async_computation.1 | async-start | bytes 4194304 | tf_op jit(solution)/shard_map/all_to_all | solution.py:91
  74.5 22.1 %all-to-all-start.2 = ((f32[32,8,128]{2,1,0:T(8,128)}), f32[32,8,128]{2,1,0:T(8,128)S(1)}, u32[]{:S(2)}, u32[]{:S(2)}) async-start(f32[32,8,128]{2,1,0:T(8,128)} %shard_map.46), calls=%async_computation.2 | async-start | bytes 262144 | tf_op jit(solution)/shard_map/all_to_all | solution.py:94

commit v3 on v2

--- a/solution.py
+++ b/solution.py
@@ -16,15 +16,116 @@
     return jnp.dot(a, b, precision=highest, preferred_element_type=jnp.float32)
 
 
+def parted(a):
+    high = a.astype(jnp.bfloat16)
+    rest = a - high.astype(jnp.float32)
+    middle = rest.astype(jnp.bfloat16)
+    return high, middle, (rest - middle.astype(jnp.float32)).astype(jnp.bfloat16)
+
+
+def narrow(a, b, across):
+    return lax.dot_general(a, b, (((1,), (across,)), ((), ())), preferred_element_type=jnp.float32)
+
+
+def thin_dot(a, parts, across):
+    high, middle, low = parts
+    rows = a[0].shape[0]
+    first = narrow(jnp.concatenate(a, axis=0), high, across)
+    second = narrow(jnp.concatenate(a[:2], axis=0), middle, across)
+    third = narrow(a[0], low, across)
+    small = first[2 * rows :] + second[rows:] + third
+    return first[:rows] + (first[rows : 2 * rows] + second[:rows] + small)
+
+
+def lower_rows(shape):
+    return lax.broadcasted_iota(jnp.int32, shape, len(shape) - 2) < shape[-2] // 2
+
+
+def share_kernel(given_ref, lined_ref, hole_ref, share_ref, given, lined, hole, padded, arrived):
+    own, cols, _ = given.shape
+    norbs = hole.shape[0]
+    blocks = 2 * share_ref.shape[0]
+    occs = norbs // own
+    kept = norbs // blocks
+    half = lined.shape[0] // 2
+    copies = [
+        pltpu.make_async_copy(given_ref, given, arrived.at[0]),
+        pltpu.make_async_copy(hole_ref, hole, arrived.at[1]),
+    ]
+    for c in range(2):
+        rows = pl.ds(c * half, half)
+        copies.append(pltpu.make_async_copy(lined_ref.at[rows, :], lined.at[rows, :], arrived.at[2 + c]))
+    for copy in copies:
+        copy.start()
+    padded[...] = jnp.zeros_like(padded)
+    place = lax.broadcasted_iota(jnp.int32, (blocks * cols * kept, norbs), 0)
+    device, inner = place // (cols * kept), place % (cols * kept)
+    wanted = (device % occs) * own + (device // occs) * kept + inner % kept
+    index = lax.broadcasted_iota(jnp.int32, (blocks * cols * kept, norbs), 1)
+    square = (norbs, norbs)
+    unit = lax.broadcasted_iota(jnp.int32, square, 0) == lax.broadcasted_iota(jnp.int32, square, 1)
+    first = pl.multiple_of(lax.axis_index("occ") * own, own)
+    copies[0].wait()
+    copies[1].wait()
+    dress = jnp.where(unit, 1.0, 0.0) - hole[...]
+    total = None
+    for j in range(cols):
+        padded[j, pl.ds(first, own), :] = given[:, j, :]
+        dressed = dot(dress, padded[j])
+        chosen = jnp.where((wanted == index) & (inner // kept == j), 1.0, 0.0)
+        term = dot(chosen, dressed)
+        total = term if j == 0 else total + term
+    total = parted(total)
+    found = []
+    for c in range(2):
+        copies[2 + c].wait()
+        term = thin_dot(total, parted(lined[c * half : (c + 1) * half, :]), 1)
+        found.append(term.reshape(blocks // 2, 2 * cols * kept, half))
+    lower = lower_rows(found[0].shape)
+    turned = [pltpu.roll(term, cols * kept, 1) for term in found]
+    share_ref[:, 0] = jnp.where(lower, found[0], turned[1])
+    share_ref[:, 1] = jnp.where(lower, turned[0], found[1])
+
+
+def share_of(given, lined, hole, blocks):
+    naux = lined.shape[0]
+    rows = 2 * given.shape[1] * hole.shape[0] // blocks
+    return pl.pallas_call(
+        share_kernel,
+        out_shape=jax.ShapeDtypeStruct((blocks // 2, 2, rows, naux // 2), jnp.float32),
+        in_specs=[pl.BlockSpec(memory_space=pl.ANY)] * 3,
+        out_specs=pl.BlockSpec(memory_space=pltpu.VMEM),
+        scratch_shapes=[
+            pltpu.VMEM(given.shape, jnp.float32),
+            pltpu.VMEM(lined.shape, jnp.float32),
+            pltpu.VMEM(hole.shape, jnp.float32),
+            pltpu.VMEM((given.shape[1], hole.shape[0], given.shape[2]), jnp.float32),
+            pltpu.SemaphoreType.DMA((4,)),
+        ],
+    )(given, lined, hole)
+
+
 def contract_kernel(fitted_ref, factors_ref, ladder_ref):
-    total = dot(fitted_ref[...], factors_ref[...])
+    halves, rows, half = fitted_ref.shape
+    found = fitted_ref[...].reshape(halves // 2, 2, rows, half)
+    even, odd = found[:, 0], found[:, 1]
+    lower = lower_rows(even.shape)
+    parts = (
+        jnp.where(lower, even, pltpu.roll(odd, rows // 2, 1)),
+        jnp.where(lower, pltpu.roll(even, rows // 2, 1), odd),
+    )
+    total = None
+    for c in range(2):
+        fitted = parted(parts[c].reshape(halves * rows // 2, half))
+        term = thin_dot(fitted, parted(factors_ref[c * half : (c + 1) * half, :]), 0)
+        total = term if c == 0 else total + term
     blocks, rows, _ = ladder_ref.shape
     turned = total.T.reshape(blocks, 2, rows, total.shape[0])
     ladder_ref[...] = jnp.concatenate([turned[:, 0], turned[:, 1]], axis=-1)
 
 
 def contract(fitted, factors, blocks):
-    cols, pairs = fitted.shape[0], factors.shape[1]
+    cols, pairs = fitted.shape[0] * fitted.shape[1] // 2, factors.shape[1]
     return pl.pallas_call(
         contract_kernel,
         out_shape=jax.ShapeDtypeStruct((blocks, pairs // blocks // 2, 2 * cols), jnp.float32),
@@ -67,22 +168,16 @@
     naux = fit_con.shape[0]
     halves, lots = lax.axis_size("out_hi"), lax.axis_size("out_lo")
     cons, occs = lax.axis_size("con"), lax.axis_size("occ")
-    own, cols = amplitudes.shape[1], amplitudes.shape[2]
+    cols = amplitudes.shape[2]
     kept = norbs // (cons * occs)
     side = lax.axis_index("out_lo")
     dress = jnp.eye(norbs, dtype=jnp.float32) - hole_hole
 
-    first = lax.axis_index("occ") * own
-    columns = lax.dynamic_slice_in_dim(dress, first, own, 1)
-    columns = jnp.swapaxes(columns.reshape(occs, cons, kept, own), 0, 1).reshape(norbs, own)
-    half = jnp.einsum("im,qmj->ijq", columns, amplitudes, precision=highest)
-    half = half.reshape(norbs * cols, half.shape[2])
-    share = jnp.einsum("pq,lq->pl", half, fit_con, precision=highest)
-    share = share.reshape(cons * occs, kept * cols, naux)
+    share = share_of(jnp.transpose(amplitudes, (1, 2, 0)), fit_con, hole_hole, cons * occs)
+    share = share.reshape(cons * occs, *share.shape[2:])
     parts = lax.all_to_all(share, plane, 0, 0, tiled=True)
     fitted = jnp.sum(parts, axis=0)
     whole = lax.all_gather(fitted, "out_hi", axis=0)
-    whole = whole.reshape(halves * kept * cols, naux)
     other = lax.ppermute(fit_out, "out_lo", [(0, 1), (1, 0)])
     factors = jnp.concatenate(
         [jnp.where(side == 0, fit_out, other), jnp.where(side == 0, other, fit_out)], axis=1
@@ -96,9 +191,9 @@
     ladder = ladder.reshape(lots, cons * rows // 2, lanes)
     orders = jnp.swapaxes(dress.T.reshape(halves, lots, cols, norbs), 0, 1)
     orders = jnp.pad(orders, ((0, 0), (0, 0), (0, 0), (0, lanes - norbs)))
-    orders = orders.reshape(lots, 1, halves, 1, cols, 1, 1, lanes)
+    orders = orders.reshape(lots, 1, halves, cols, 1, 1, 1, lanes)
     same = jnp.eye(2, dtype=jnp.float32).reshape(1, 2, 1, 1, 1, 2, 1, 1)
-    kind = jnp.eye(kept, dtype=jnp.float32).reshape(1, 1, 1, kept, 1, 1, kept, 1)
+    kind = jnp.eye(kept, dtype=jnp.float32).reshape(1, 1, 1, 1, kept, 1, kept, 1)
     blocks = (orders * same * kind).reshape(lots, lanes, 2 * kept * lanes)
     return finish(ladder, blocks, (rows, cons * kept, norbs), kept)
 

time: 98.3 us -> 97.1 us (0.988)
  Pallas kernels: 3.44 us -> 6.1 us
  matrix products: 1.54 us -> 0 us
  local copies, waits for them, and re-layouts: 4 us -> 2.63 us
    pallas_call x0 -> x1, Pallas kernels: none -> 3.2 us  [share_of(): pl.pallas_call(share_kernel, out_shape=jax.ShapeDtypeStruct((blocks // 2,...]
    dot_general x2 -> x0, matrix products: 1.54 us -> none  [the longest x1 0.95 us: local(): half = jnp.einsum('im,qmj->ijq', columns, amplitudes, precision=highest)]
    dot_general x1 -> x0, local copies, waits for them, and re-layouts: 1.14 us -> none  [local(): share = jnp.einsum('pq,lq->pl', half, fit_con, precision=highest)]
where the time goes in v3:
time: 97.1 us; the launch traced here: 96.7 us
  starting transfers between devices  38.5 us (40%)
  blocking collectives  33.5 us (35%)
  waiting for transfers between devices  15.6 us (16%)
  Pallas kernels  6.1 us (6%)
  local copies, waits for them, and re-layouts  2.63 us (3%)
    all_gather x1, blocking collectives, local(): whole = lax.all_gather(fitted, 'out_hi', axis=0)  33.5 us
    all_to_all x1, starting transfers between devices, local(): parts = lax.all_to_all(share, plane, 0, 0, tiled=True)  17.7 us
    all_to_all x1, starting transfers between devices, local(): ladder = lax.all_to_all(ladder, pair, 0, 0, tiled=True)  13.7 us
    all_to_all x1, waiting for transfers between devices, local(): ladder = lax.all_to_all(ladder, pair, 0, 0, tiled=True)  7.12 us
    all_to_all x1, starting transfers between devices, local(): factors = lax.all_to_all(factors, 'con', 0, 0, tiled=True)  5.22 us
    all_to_all x1, waiting for transfers between devices, local(): parts = lax.all_to_all(share, plane, 0, 0, tiled=True)  5.13 us
    ppermute x1, waiting for transfers between devices, local(): other = lax.ppermute(fit_out, 'out_lo', [(0, 1), (1, 0)])  3.37 us
    pallas_call x1, Pallas kernels, share_of(): pl.pallas_call(share_kernel, out_shape=jax.ShapeDtypeStruct((blocks // 2,...  3.2 us
  transfers between devices with their start and end apart: 4, of which 3 were waited for; matrix products, arithmetic and copies ran while one was open for 1% of the time, Pallas kernels for 0%

profile of v3, /device:TPU:1, one launch (start us, length us, event | category | flops | bytes accessed | tf_op | source)
XLA Modules:
  0.0 96.7 jit_solution(1988742194633792125)
XLA Ops:
  0.0 0.0 copy-start.1
  0.0 3.2 %shard_map.46 = f32[16,2,8,512]{3,2,1,0:T(8,128)} custom-call(f32[32,2,128]{2,1,0:T(2,128)} %bitcast.15, f32[1024,128]{1,0:T(8,128)} %lined_ref.1, f32[64,64]{1,0:T(8,128)} %hole_ref.1), custom_call_target="tpu_custom_call" | custom-call | tf_op jit(solution)/shard_map/pallas_call | solution.py:93
  3.2 17.7 %all-to-all-start = ((f32[32,8,512]{2,1,0:T(8,128)}), f32[32,8,512]{2,1,0:T(8,128)S(1)}, u32[]{:S(2)}, u32[]{:S(2)}) async-start(f32[32,8,512]{2,1,0:T(8,128)} %bitcast.13), calls=%async_computation | async-start | bytes 1048576 | tf_op jit(solution)/shard_map/all_to_all | solution.py:178
  20.9 0.0 copy-done.1
  20.9 1.9 %collective-permute-start = (f32[64,256]{1,0:T(8,128)S(1)}, f32[64,256]{1,0:T(8,128)S(1)}, u32[]{:S(2)}, u32[]{:S(2)}) collective-permute-start(f32[64,256]{1,0:T(8,128)S(1)} %copy-done.1), channel_id=1, source_target_pairs={{0,32},{32,0},{1,33},{33,1},{2,34},{34,2},{3,35},{35,3},{4,36},{36... | collective-permute-start | bytes 196616 | tf_op jit(solution)/shard_map/ppermute | solution.py:181
  22.8 3.4 %collective-permute-done = f32[64,256]{1,0:T(8,128)S(1)} collective-permute-done((f32[64,256]{1,0:T(8,128)S(1)}, f32[64,256]{1,0:T(8,128)S(1)}, u32[]{:S(2)}, u32[]{:S(2)}) %collective-permute-start) | collective-permute-done | bytes 65568 | tf_op jit(solution)/shard_map/ppermute | solution.py:181
  26.2 5.1 %all-to-all-done = f32[32,8,512]{2,1,0:T(8,128)S(1)} async-done(((f32[32,8,512]{2,1,0:T(8,128)}), f32[32,8,512]{2,1,0:T(8,128)S(1)}, u32[]{:S(2)}, u32[]{:S(2)}) %all-to-all-start) | async-done | bytes 524320 | tf_op jit(solution)/shard_map/all_to_all | solution.py:178
  31.4 1.6 %broadcast_in_dim.2 = f32[16,64,512]{2,1,0:T(8,128)} broadcast(f32[64,512]{1,0:T(8,128)S(1)} %pad_maximum_fusion), dimensions={1,2} | broadcast | bytes 2228224 | tf_op jit(solution)/shard_map/broadcast_in_dim | solution.py:185
  33.0 5.2 %all-to-all-start.1 = ((f32[16,64,512]{2,1,0:T(8,128)}), f32[16,64,512]{2,1,0:T(8,128)S(1)}, u32[]{:S(2)}, u32[]{:S(2)}) async-start(f32[16,64,512]{2,1,0:T(8,128)} %broadcast_in_dim.2), calls=%async_computation.1 | async-start | bytes 4194304 | tf_op jit(solution)/shard_map/all_to_all | solution.py:186
  38.2 0.0 copy-start
  38.3 33.5 %all-gather = f32[128,512]{1,0:T(8,128)S(1)} all-gather(f32[8,512]{1,0:T(8,128)S(1)} %reduce_sum.9), channel_id=2, replica_groups=mesh['out_hi'=16,'out_lo'=2,'con'=16,'occ'=2] {'out_hi'}, dimensions={0}, use_global_device_ids=true | all-gather | bytes 278528 | tf_op jit(solution)/shard_map/all_gather | solution.py:180
  71.7 0.0 all-to-all-done.1
  71.7 1.6 %shard_map.47 = f32[32,8,128]{2,1,0:T(8,128)} custom-call(f32[16,8,512]{2,1,0:T(8,128)S(1)} %bitcast.11, f32[1024,512]{1,0:T(8,128)S(1)} %bitcast.10), custom_call_target="tpu_custom_call" | custom-call | tf_op jit(solution)/shard_map/pallas_call | solution.py:129
  73.3 13.7 %all-to-all-start.2 = ((f32[32,8,128]{2,1,0:T(8,128)}), f32[32,8,128]{2,1,0:T(8,128)S(1)}, u32[]{:S(2)}, u32[]{:S(2)}) async-start(f32[32,8,128]{2,1,0:T(8,128)} %shard_map.47), calls=%async_computation.2 | async-start | bytes 262144 | tf_op jit(solution)/shard_map/all_to_all | solution.py:189
  87.0 0.0 copy-done
  87.0 0.1 copy.6
  87.1 0.1 broadcast_multiply_fusion.1
  87.3 0.1 mul.41
  87.4 0.4 mul.42
  87.8 0.1 mul.43
  88.0 0.2 mul.44
  88.2 0.1 broadcast_multiply_fusion.blocks_ref
  88.3 7.1 %all-to-all-done.2 = f32[32,8,128]{2,1,0:T(8,128)S(1)} async-done(((f32[32,8,128]{2,1,0:T(8,128)}), f32[32,8,128]{2,1,0:T(8,128)S(1)}, u32[]{:S(2)}, u32[]{:S(2)}) %all-to-all-start.2) | async-done | bytes 131104 | tf_op jit(solution)/shard_map/all_to_all | solution.py:189
  95.4 1.3 %shard_map.48 = f32[16,32,64]{2,1,0:T(8,128)} custom-call(f32[2,128,128]{2,1,0:T(8,128)S(1)} %bitcast.12, f32[2,128,512]{2,1,0:T(8,128)S(1)} %broadcast_multiply_fusion.blocks_ref), custom_call_target="tpu_custom_call" | custom-call | tf_op jit(solution)/shard_map/pallas_call | solution.py:156
  (7 shorter events, 0.1 us)
Async XLA Ops:
  0.0 20.9 %copy-start.1 = (f32[64,256]{1,0:T(8,128)S(1)}, f32[64,256]{1,0:T(8,128)}, u32[]{:S(2)}) copy-start(f32[64,256]{1,0:T(8,128)} %param.5) | copy-start | bytes 196612
  3.2 28.2 %all-to-all-start = ((f32[32,8,512]{2,1,0:T(8,128)}), f32[32,8,512]{2,1,0:T(8,128)S(1)}, u32[]{:S(2)}, u32[]{:S(2)}) async-start(f32[32,8,512]{2,1,0:T(8,128)} %bitcast.13), calls=%async_computation | async-start | bytes 1048576 | tf_op jit(solution)/shard_map/all_to_all | solution.py:178
  20.9 5.3 %collective-permute-start = (f32[64,256]{1,0:T(8,128)S(1)}, f32[64,256]{1,0:T(8,128)S(1)}, u32[]{:S(2)}, u32[]{:S(2)}) collective-permute-start(f32[64,256]{1,0:T(8,128)S(1)} %copy-done.1), channel_id=1, source_target_pairs={{0,32},{32,0},{1,33},{33,1},{2,34},{34,2},{3,35},{35,3},{4,36},{36... | collective-permute-start | bytes 196616 | tf_op jit(solution)/shard_map/ppermute | solution.py:181
  33.0 38.7 %all-to-all-start.1 = ((f32[16,64,512]{2,1,0:T(8,128)}), f32[16,64,512]{2,1,0:T(8,128)S(1)}, u32[]{:S(2)}, u32[]{:S(2)}) async-start(f32[16,64,512]{2,1,0:T(8,128)} %broadcast_in_dim.2), calls=%async_computation.1 | async-start | bytes 4194304 | tf_op jit(solution)/shard_map/all_to_all | solution.py:186
  38.2 48.8 %copy-start = (f32[64,64]{1,0:T(8,128)S(1)}, f32[64,64]{1,0:T(8,128)}, u32[]{:S(2)}) copy-start(f32[64,64]{1,0:T(8,128)} %hole_ref.1) | copy-start | bytes 49156
  73.3 22.1 %all-to-all-start.2 = ((f32[32,8,128]{2,1,0:T(8,128)}), f32[32,8,128]{2,1,0:T(8,128)S(1)}, u32[]{:S(2)}, u32[]{:S(2)}) async-start(f32[32,8,128]{2,1,0:T(8,128)} %shard_map.47), calls=%async_computation.2 | async-start | bytes 262144 | tf_op jit(solution)/shard_map/all_to_all | solution.py:189

commit v4 on v3

v4 whole, which is shorter than its diff:
```python
import jax
import jax.numpy as jnp
from jax import lax
from jax.experimental import pallas as pl
from jax.experimental.pallas import tpu as pltpu
from jax.sharding import Mesh, PartitionSpec as P

highest = lax.Precision.HIGHEST
con = ("row", "core")
near = ("out_mid", "out_lo")
group = ("out_mid", *con, "occ")
back = (*near, "row")
lanes = 128
room = 16 * 1024 * 1024


def dot(a, b):
    return jnp.dot(a, b, precision=highest, preferred_element_type=jnp.float32)


def parted(a):
    high = a.astype(jnp.bfloat16)
    rest = a - high.astype(jnp.float32)
    middle = rest.astype(jnp.bfloat16)
    return high, middle, (rest - middle.astype(jnp.float32)).astype(jnp.bfloat16)


def narrow(a, b, across):
    return lax.dot_general(a, b, (((1,), (across,)), ((), ())), preferred_element_type=jnp.float32)


def thin_dot(a, parts, across):
    high, middle, low = parts
    rows = a[0].shape[0]
    first = narrow(jnp.concatenate(a, axis=0), high, across)
    second = narrow(jnp.concatenate(a[:2], axis=0), middle, across)
    third = narrow(a[0], low, across)
    small = first[2 * rows :] + second[rows:] + third
    return first[:rows] + (first[rows : 2 * rows] + second[:rows] + small)


def lower_rows(shape):
    return lax.broadcasted_iota(jnp.int32, shape, len(shape) - 2) < shape[-2] // 2


def share_kernel(given_ref, lined_ref, hole_ref, share_ref, given, lined, hole, padded, arrived):
    own, cols, _ = given.shape
    norbs = hole.shape[0]
    blocks = 2 * share_ref.shape[1]
    occs = norbs // own
    kept = norbs // blocks
    sides, cons, depth, width = lined.shape
    quarter = cons * depth // 2
    copies = [
        pltpu.make_async_copy(given_ref, given, arrived.at[0]),
        pltpu.make_async_copy(hole_ref, hole, arrived.at[1]),
    ]
    for c in range(sides):
        copies.append(pltpu.make_async_copy(lined_ref.at[:, c], lined.at[c], arrived.at[2 + c]))
    for copy in copies:
        copy.start()
    padded[...] = jnp.zeros_like(padded)
    place = lax.broadcasted_iota(jnp.int32, (blocks * cols * kept, norbs), 0)
    device, inner = place // (cols * kept), place % (cols * kept)
    wanted = (device % occs) * own + (device // occs) * kept + inner % kept
    index = lax.broadcasted_iota(jnp.int32, (blocks * cols * kept, norbs), 1)
    square = (norbs, norbs)
    unit = lax.broadcasted_iota(jnp.int32, square, 0) == lax.broadcasted_iota(jnp.int32, square, 1)
    first = pl.multiple_of(lax.axis_index("occ") * own, own)
    copies[0].wait()
    copies[1].wait()
    dress = jnp.where(unit, 1.0, 0.0) - hole[...]
    total = None
    for j in range(cols):
        padded[j, pl.ds(first, own), :] = given[:, j, :]
        dressed = dot(dress, padded[j])
        chosen = jnp.where((wanted == index) & (inner // kept == j), 1.0, 0.0)
        term = dot(chosen, dressed)
        total = term if j == 0 else total + term
    total = parted(total)
    for c in range(sides):
        copies[2 + c].wait()
        known = lined[c].reshape(2 * quarter, width)
        found = []
        for q in range(2):
            term = thin_dot(total, parted(known[q * quarter : (q + 1) * quarter]), 1)
            found.append(term.reshape(blocks // 2, 2 * cols * kept, quarter))
        lower = lower_rows(found[0].shape)
        turned = [pltpu.roll(term, cols * kept, 1) for term in found]
        share_ref[c, :, 0] = jnp.where(lower, found[0], turned[1])
        share_ref[c, :, 1] = jnp.where(lower, turned[0], found[1])


def share_of(given, lined, hole, blocks):
    sides, quarter = lined.shape[1], lined.shape[0] * lined.shape[2] // 2
    rows = 2 * given.shape[1] * hole.shape[0] // blocks
    return pl.pallas_call(
        share_kernel,
        out_shape=jax.ShapeDtypeStruct((sides, blocks // 2, 2, rows, quarter), jnp.float32),
        in_specs=[pl.BlockSpec(memory_space=pl.ANY)] * 3,
        out_specs=pl.BlockSpec(memory_space=pltpu.VMEM),
        scratch_shapes=[
            pltpu.VMEM(given.shape, jnp.float32),
            pltpu.VMEM((sides, lined.shape[0], *lined.shape[2:]), jnp.float32),
            pltpu.VMEM(hole.shape, jnp.float32),
            pltpu.VMEM((given.shape[1], hole.shape[0], given.shape[2]), jnp.float32),
            pltpu.SemaphoreType.DMA((4,)),
        ],
    )(given, lined, hole)


def contract_kernel(fitted_ref, factors_ref, ladder_ref):
    halves, rows, half = fitted_ref.shape
    found = fitted_ref[...].reshape(halves // 2, 2, rows, half)
    even, odd = found[:, 0], found[:, 1]
    lower = lower_rows(even.shape)
    parts = (
        jnp.where(lower, even, pltpu.roll(odd, rows // 2, 1)),
        jnp.where(lower, pltpu.roll(even, rows // 2, 1), odd),
    )
    total = None
    for c in range(2):
        fitted = parted(parts[c].reshape(halves * rows // 2, half))
        term = thin_dot(fitted, parted(factors_ref[c * half : (c + 1) * half, :]), 0)
        total = term if c == 0 else total + term
    ladder_ref[...] = total.T.reshape(ladder_ref.shape)


def contract(fitted, factors, blocks):
    cols, pairs = fitted.shape[0] * fitted.shape[1] // 2, factors.shape[1]
    return pl.pallas_call(
        contract_kernel,
        out_shape=jax.ShapeDtypeStruct((blocks, pairs // blocks, cols), jnp.float32),
        in_specs=[pl.BlockSpec(memory_space=pltpu.VMEM)] * 2,
        out_specs=pl.BlockSpec(memory_space=pltpu.VMEM),
        compiler_params=pltpu.CompilerParams(vmem_limit_bytes=room),
    )(fitted, factors)


def finish_kernel(ladder_ref, blocks_ref, out_ref, held):
    lots = blocks_ref.shape[0]
    total = None
    for z in range(lots):
        term = thin_dot(parted(ladder_ref[0, z] + ladder_ref[1, z]), parted(blocks_ref[z]), 0)
        total = term if z == 0 else total + term
    kinds = held.shape[0]
    rows, _, norbs = out_ref.shape
    lines = out_ref.shape[1] // kinds
    for s in range(kinds):
        held[s] = total[:, s * lanes : (s + 1) * lanes]
    for s in range(kinds):
        for r in range(rows):
            line = held[s, pl.ds(r, lines, stride=rows), :]
            out_ref[r, pl.ds(s, lines, stride=kinds), :] = line[:, :norbs]


def finish(ladder, blocks, shape):
    kinds = blocks.shape[2] // lanes
    return pl.pallas_call(
        finish_kernel,
        out_shape=jax.ShapeDtypeStruct(shape, jnp.float32),
        in_specs=[pl.BlockSpec(memory_space=pltpu.VMEM)] * 2,
        out_specs=pl.BlockSpec(memory_space=pltpu.VMEM),
        scratch_shapes=[pltpu.VMEM((kinds, ladder.shape[2], lanes), jnp.float32)],
        compiler_params=pltpu.CompilerParams(vmem_limit_bytes=room),
    )(ladder, blocks)


def exchanged(array, flip):
    return lax.ppermute(array, near, [(k, k ^ flip) for k in range(4)])


def local(amplitudes, fit_out, fit_con, hole_hole):
    norbs = hole_hole.shape[0]
    naux = fit_con.shape[0]
    highs, mids, lots = lax.axis_size("out_hi"), lax.axis_size("out_mid"), lax.axis_size("out_lo")
    lines, cores, occs = lax.axis_size("row"), lax.axis_size("core"), lax.axis_size("occ")
    cons = lines * cores
    cols = amplitudes.shape[2]
    kept = norbs // (cons * occs)
    pairs = fit_out.shape[1]
    rows = pairs // cons
    depth = naux // cons // mids
    mid, low = lax.axis_index("out_mid"), lax.axis_index("out_lo")
    dress = jnp.eye(norbs, dtype=jnp.float32) - hole_hole

    lined = fit_con.reshape(cons, mids, depth, fit_con.shape[1])
    share = share_of(jnp.transpose(amplitudes, (1, 2, 0)), lined, hole_hole, cons * occs)
    share = share.reshape(mids * cons * occs, *share.shape[3:])
    parts = lax.all_to_all(share, group, 0, 0, tiled=True)
    parts = parts.reshape(mids, cons * occs, *parts.shape[1:])
    fitted = jnp.sum(parts, axis=1).reshape(-1, parts.shape[3])
    whole = lax.all_gather(fitted, ("out_hi", "core"), axis=0)
    whole = whole.reshape(highs * cores * mids, -1, whole.shape[2])
    index = jnp.arange(pairs)
    origin = (index // rows % lines * cores + index // (rows * lines)) * rows + index % rows
    chosen = (index[:, None] == origin[None]).astype(jnp.float32)
    mine = jnp.dot(fit_out, chosen, precision=highest).reshape(mids, depth, pairs)
    near_half = jnp.where(mid == 0, mine[0], mine[1])
    far_half = jnp.where(mid == 0, mine[1], mine[0])
    found = [near_half, exchanged(near_half, 1), exchanged(far_half, 2), exchanged(far_half, 3)]
    found = [jnp.where(low == 0, found[k], found[k ^ 1]) for k in range(4)]
    found = [jnp.where(mid == 0, found[k], found[k ^ 2]) for k in range(4)]
    wide = pairs // cores
    factors = jnp.stack(
        [jnp.concatenate([p[:, c * wide : (c + 1) * wide] for p in found], axis=1) for c in range(cores)]
    )
    factors = jnp.broadcast_to(factors[None], (lines, *factors.shape))
    factors = lax.all_to_all(factors.reshape(cons, *factors.shape[2:]), con, 0, 0, tiled=True)
    factors = factors.reshape(cons * depth, mids * lots * wide)
    ladder = contract(whole, factors, mids * lots * lines)
    ladder = lax.all_to_all(ladder, back, 0, 0, tiled=True)
    ladder = ladder.reshape(mids, lots, lines * rows, lanes)
    orders = jnp.transpose(dress.T.reshape(highs, mids, lots, cols, norbs), (2, 0, 1, 3, 4))
    orders = jnp.pad(orders, ((0, 0),) * 4 + ((0, lanes - norbs),))
    orders = orders.reshape(lots, highs, 1, mids, cols, 1, 1, 1, lanes)
    same = jnp.eye(cores, dtype=jnp.float32).reshape(1, 1, cores, 1, 1, 1, cores, 1, 1)
    kind = jnp.eye(kept, dtype=jnp.float32).reshape(1, 1, 1, 1, 1, kept, 1, kept, 1)
    blocks = (orders * same * kind).reshape(lots, lanes, cores * kept * lanes)
    return finish(ladder, blocks, (rows, cons * kept, norbs))


def solution(mesh):
    shape = dict(mesh.shape)
    sizes = (shape["out"] // 4, 2, 2, shape["con"] // 2, 2, shape["occ"])
    finer = Mesh(mesh.devices.reshape(sizes), ("out_hi", *near, *con, "occ"))
    out = ("out_hi", *near)
    return jax.shard_map(
        local,
        mesh=finer,
        in_specs=(P(con, "occ", out), P(con, out), P(None, con), P()),
        out_specs=P((*out, *con), "occ", None),
        check_vma=False,
    )
```

time: 97.1 us -> 101 us (1.040)
  starting transfers between devices: 38.5 us -> 42.4 us
  blocking collectives: 33.5 us -> 34.6 us
    ppermute x1 -> x3, starting transfers between devices: 1.92 us -> 9.39 us  [exchanged(): return lax.ppermute(array, near, [(k, k ^ flip) for k in range(4)])]
    all_to_all x3, starting transfers between devices: 36.6 us -> 33 us  [the longest x1 18.2 us: local(): parts = lax.all_to_all(share, group, 0, 0, tiled=True)]
    all_gather x1, blocking collectives: 33.5 us -> 34.6 us  [local(): whole = lax.all_gather(fitted, ('out_hi', 'core'), axis=0)]
    ppermute x1 -> x3, waiting for transfers between devices: 3.37 us -> 3.38 us  [exchanged(): return lax.ppermute(array, near, [(k, k ^ flip) for k in range(4)])]
  transfers between devices with their start and end apart: 4 -> 6, of which waited for: 3 -> 5; matrix products, arithmetic and copies ran while one was open for 1% -> 2% of each run, Pallas kernels for 0% -> 0%
where the time goes in v4:
time: 101 us
  starting transfers between devices  42.4 us (42%)
  blocking collectives  34.6 us (34%)
  waiting for transfers between devices  15.2 us (15%)
  Pallas kernels  5.77 us (6%)
  local copies, waits for them, and re-layouts  2.18 us (2%)
    all_gather x1, blocking collectives, local(): whole = lax.all_gather(fitted, ('out_hi', 'core'), axis=0)  34.6 us
    all_to_all x1, starting transfers between devices, local(): parts = lax.all_to_all(share, group, 0, 0, tiled=True)  18.2 us
    all_to_all x1, waiting for transfers between devices, local(): ladder = lax.all_to_all(ladder, back, 0, 0, tiled=True)  10.8 us
    ppermute x3, starting transfers between devices, exchanged(): return lax.ppermute(array, near, [(k, k ^ flip) for k in range(4)])  9.39 us
    all_to_all x1, starting transfers between devices, local(): lax.all_to_all(factors.reshape(cons, *factors.shape[2:]), con, 0, 0, tile...  7.58 us
    all_to_all x1, starting transfers between devices, local(): ladder = lax.all_to_all(ladder, back, 0, 0, tiled=True)  7.21 us
    ppermute x3, waiting for transfers between devices, exchanged(): return lax.ppermute(array, near, [(k, k ^ flip) for k in range(4)])  3.38 us
    pallas_call x1, Pallas kernels, share_of(): pl.pallas_call(share_kernel, out_shape=jax.ShapeDtypeStruct((sides, block...  3.03 us
  transfers between devices with their start and end apart: 6, of which 5 were waited for; matrix products, arithmetic and copies ran while one was open for 2% of the time, Pallas kernels for 0%

profile of v4, /device:TPU:1, one launch (start us, length us, event | category | flops | bytes accessed | tf_op | source)
XLA Modules:
  0.0 100.8 jit_solution(16905461095718892928)
XLA Ops:
  0.0 0.0 copy-start
  0.0 3.0 %shard_map.46 = f32[2,16,2,8,256]{4,3,2,1,0:T(8,128)} custom-call(f32[32,2,128]{2,1,0:T(2,128)} %bitcast.29, f32[16,2,32,128]{3,2,1,0:T(8,128)} %bitcast.26, f32[64,64]{1,0:T(8,128)} %hole_ref.1), custom_call_target="tpu_custom_call" | custom-call | tf_op jit(solution)/shard_map/pallas_call | solution.py:97
  3.0 18.2 %all-to-all-start = ((f32[64,8,256]{2,1,0:T(8,128)}), f32[64,8,256]{2,1,0:T(8,128)S(1)}, u32[]{:S(2)}, u32[]{:S(2)}) async-start(f32[64,8,256]{2,1,0:T(8,128)} %bitcast.25), calls=%async_computation | async-start | bytes 1048576 | tf_op jit(solution)/shard_map/all_to_all | solution.py:190
  21.3 0.0 copy-done
  21.3 0.2 convolution_bitcast_fusion
  21.5 1.9 %collective-permute-start = (f32[32,256]{1,0:T(8,128)S(1)}, f32[32,256]{1,0:T(8,128)S(1)}, u32[]{:S(2)}, u32[]{:S(2)}) collective-permute-start(f32[32,256]{1,0:T(8,128)S(1)} %get-tuple-element.10), channel_id=1, source_target_pairs={{0,32},{32,0},{64,96},{96,64},{1,33},{33,1},{65,97},{97,65},{2,34}... | collective-permute-start | bytes 98312 | tf_op jit(solution)/shard_map/ppermute | solution.py:170
  23.4 4.4 %collective-permute-start.1 = (f32[32,256]{1,0:T(8,128)S(1)}, f32[32,256]{1,0:T(8,128)S(1)}, u32[]{:S(2)}, u32[]{:S(2)}) collective-permute-start(f32[32,256]{1,0:T(8,128)S(1)} %get-tuple-element.9), channel_id=1, source_target_pairs={{0,64},{32,96},{64,0},{96,32},{1,65},{33,97},{65,1},{97,33},{2,66}... | collective-permute-start | bytes 98312 | tf_op jit(solution)/shard_map/ppermute | solution.py:170
  27.8 3.1 %collective-permute-start.2 = (f32[32,256]{1,0:T(8,128)S(1)}, f32[32,256]{1,0:T(8,128)S(1)}, u32[]{:S(2)}, u32[]{:S(2)}) collective-permute-start(f32[32,256]{1,0:T(8,128)S(1)} %get-tuple-element.9), channel_id=1, source_target_pairs={{0,96},{32,64},{64,32},{96,0},{1,97},{33,65},{65,33},{97,1},{2,98}... | collective-permute-start | bytes 98312 | tf_op jit(solution)/shard_map/ppermute | solution.py:170
  30.9 0.8 collective-permute-done
  31.7 0.3 collective-permute-done.1
  32.0 2.3 %collective-permute-done.2 = f32[32,256]{1,0:T(8,128)S(1)} collective-permute-done((f32[32,256]{1,0:T(8,128)S(1)}, f32[32,256]{1,0:T(8,128)S(1)}, u32[]{:S(2)}, u32[]{:S(2)}) %collective-permute-start.2) | collective-permute-done | bytes 32800 | tf_op jit(solution)/shard_map/ppermute | solution.py:170
  34.4 1.0 %all-to-all-done = f32[64,8,256]{2,1,0:T(8,128)S(1)} async-done(((f32[64,8,256]{2,1,0:T(8,128)}), f32[64,8,256]{2,1,0:T(8,128)S(1)}, u32[]{:S(2)}, u32[]{:S(2)}) %all-to-all-start) | async-done | bytes 524320 | tf_op jit(solution)/shard_map/all_to_all | solution.py:190
  35.4 1.1 %broadcast_in_dim.2 = f32[8,2,32,512]{3,2,1,0:T(8,128)} broadcast(f32[2,32,512]{2,1,0:T(8,128)S(1)} %pad_maximum_fusion), dimensions={1,2,3} | broadcast | bytes 1179648 | tf_op jit(solution)/shard_map/broadcast_in_dim | solution.py:208
  36.5 7.6 %all-to-all-start.1 = ((f32[16,32,512]{2,1,0:T(8,128)}), f32[16,32,512]{2,1,0:T(8,128)S(1)}, u32[]{:S(2)}, u32[]{:S(2)}) async-start(f32[16,32,512]{2,1,0:T(8,128)} %bitcast.9), calls=%async_computation.1 | async-start | bytes 2097152 | tf_op jit(solution)/shard_map/all_to_all | solution.py:209
  44.2 34.6 %all_gather.3 = f32[16,16,256]{2,1,0:T(8,128)S(1)} all-gather(f32[1,16,256]{2,1,0:T(8,128)S(1)} %bitcast.28), channel_id=1, replica_groups=mesh['out_hi'=8,'out_mid'=2,'out_lo'=2,'row'=8,'core'=2,'occ'=2] {'out_h..., dimensions={0}, use_global_device_ids=true | all-gather | bytes 278528 | tf_op jit(solution)/shard_map/all_gather | solution.py:193
  78.7 0.0 all-to-all-done.1
  78.7 1.4 %shard_map.47 = f32[32,16,128]{2,1,0:T(8,128)} custom-call(f32[32,8,256]{2,1,0:T(8,128)S(1)} %bitcast.24, f32[512,512]{1,0:T(8,128)S(1)} %bitcast.22), custom_call_target="tpu_custom_call" | custom-call | tf_op jit(solution)/shard_map/pallas_call | solution.py:131
  80.1 0.0 copy-start.1
  80.2 7.2 %all-to-all-start.2 = ((f32[32,16,128]{2,1,0:T(8,128)}), f32[32,16,128]{2,1,0:T(8,128)S(1)}, u32[]{:S(2)}, u32[]{:S(2)}) async-start(f32[32,16,128]{2,1,0:T(8,128)} %shard_map.47), calls=%async_computation.2 | async-start | bytes 524288 | tf_op jit(solution)/shard_map/all_to_all | solution.py:212
  87.4 0.0 copy-done.1
  87.4 0.1 copy.8
  87.5 0.1 broadcast_multiply_fusion.1
  87.6 0.2 mul.62
  87.8 0.4 mul.63
  88.2 0.2 mul.64
  88.4 0.2 mul.65
  88.6 0.1 broadcast_multiply_fusion.blocks_ref
  88.7 10.8 %all-to-all-done.2 = f32[32,16,128]{2,1,0:T(8,128)S(1)} async-done(((f32[32,16,128]{2,1,0:T(8,128)}), f32[32,16,128]{2,1,0:T(8,128)S(1)}, u32[]{:S(2)}, u32[]{:S(2)}) %all-to-all-start.2) | async-done | bytes 262176 | tf_op jit(solution)/shard_map/all_to_all | solution.py:212
  99.5 1.3 %shard_map.48 = f32[16,32,64]{2,1,0:T(8,128)} custom-call(f32[2,2,128,128]{3,2,1,0:T(8,128)S(1)} %bitcast.23, f32[2,128,512]{2,1,0:T(8,128)S(1)} %broadcast_multiply_fusion.blocks_ref), custom_call_target="tpu_custom_call" | custom-call | tf_op jit(solution)/shard_map/pallas_call | solution.py:159
  (13 shorter events, 0.2 us)
Async XLA Ops:
  0.0 21.3 %copy-start = (f32[64,256]{1,0:T(8,128)S(1)}, f32[64,256]{1,0:T(8,128)}, u32[]{:S(2)}) copy-start(f32[64,256]{1,0:T(8,128)} %param.5) | copy-start | bytes 196612
  3.0 32.4 %all-to-all-start = ((f32[64,8,256]{2,1,0:T(8,128)}), f32[64,8,256]{2,1,0:T(8,128)S(1)}, u32[]{:S(2)}, u32[]{:S(2)}) async-start(f32[64,8,256]{2,1,0:T(8,128)} %bitcast.25), calls=%async_computation | async-start | bytes 1048576 | tf_op jit(solution)/shard_map/all_to_all | solution.py:190
  21.5 10.2 %collective-permute-start = (f32[32,256]{1,0:T(8,128)S(1)}, f32[32,256]{1,0:T(8,128)S(1)}, u32[]{:S(2)}, u32[]{:S(2)}) collective-permute-start(f32[32,256]{1,0:T(8,128)S(1)} %get-tuple-element.10), channel_id=1, source_target_pairs={{0,32},{32,0},{64,96},{96,64},{1,33},{33,1},{65,97},{97,65},{2,34}... | collective-permute-start | bytes 98312 | tf_op jit(solution)/shard_map/ppermute | solution.py:170
  23.4 8.6 %collective-permute-start.1 = (f32[32,256]{1,0:T(8,128)S(1)}, f32[32,256]{1,0:T(8,128)S(1)}, u32[]{:S(2)}, u32[]{:S(2)}) collective-permute-start(f32[32,256]{1,0:T(8,128)S(1)} %get-tuple-element.9), channel_id=1, source_target_pairs={{0,64},{32,96},{64,0},{96,32},{1,65},{33,97},{65,1},{97,33},{2,66}... | collective-permute-start | bytes 98312 | tf_op jit(solution)/shard_map/ppermute | solution.py:170
  27.8 6.5 %collective-permute-start.2 = (f32[32,256]{1,0:T(8,128)S(1)}, f32[32,256]{1,0:T(8,128)S(1)}, u32[]{:S(2)}, u32[]{:S(2)}) collective-permute-start(f32[32,256]{1,0:T(8,128)S(1)} %get-tuple-element.9), channel_id=1, source_target_pairs={{0,96},{32,64},{64,32},{96,0},{1,97},{33,65},{65,33},{97,1},{2,98}... | collective-permute-start | bytes 98312 | tf_op jit(solution)/shard_map/ppermute | solution.py:170
  36.5 42.2 %all-to-all-start.1 = ((f32[16,32,512]{2,1,0:T(8,128)}), f32[16,32,512]{2,1,0:T(8,128)S(1)}, u32[]{:S(2)}, u32[]{:S(2)}) async-start(f32[16,32,512]{2,1,0:T(8,128)} %bitcast.9), calls=%async_computation.1 | async-start | bytes 2097152 | tf_op jit(solution)/shard_map/all_to_all | solution.py:209
  80.1 7.2 %copy-start.1 = (f32[64,64]{1,0:T(8,128)S(1)}, f32[64,64]{1,0:T(8,128)}, u32[]{:S(2)}) copy-start(f32[64,64]{1,0:T(8,128)} %hole_ref.1) | copy-start | bytes 49156
  80.2 19.3 %all-to-all-start.2 = ((f32[32,16,128]{2,1,0:T(8,128)}), f32[32,16,128]{2,1,0:T(8,128)S(1)}, u32[]{:S(2)}, u32[]{:S(2)}) async-start(f32[32,16,128]{2,1,0:T(8,128)} %shard_map.47), calls=%async_computation.2 | async-start | bytes 524288 | tf_op jit(solution)/shard_map/all_to_all | solution.py:212

commit v5 on v3

--- a/solution.py
+++ b/solution.py
@@ -6,8 +6,9 @@
 from jax.sharding import Mesh, PartitionSpec as P
 
 highest = lax.Precision.HIGHEST
-plane = ("con", "occ")
-pair = ("out_lo", "con")
+con = ("row", "core")
+plane = ("row", "core", "occ")
+pair = ("out_lo", "row")
 lanes = 128
 room = 16 * 1024 * 1024
 
@@ -119,16 +120,14 @@
         fitted = parted(parts[c].reshape(halves * rows // 2, half))
         term = thin_dot(fitted, parted(factors_ref[c * half : (c + 1) * half, :]), 0)
         total = term if c == 0 else total + term
-    blocks, rows, _ = ladder_ref.shape
-    turned = total.T.reshape(blocks, 2, rows, total.shape[0])
-    ladder_ref[...] = jnp.concatenate([turned[:, 0], turned[:, 1]], axis=-1)
+    ladder_ref[...] = total.T.reshape(ladder_ref.shape)
 
 
 def contract(fitted, factors, blocks):
     cols, pairs = fitted.shape[0] * fitted.shape[1] // 2, factors.shape[1]
     return pl.pallas_call(
         contract_kernel,
-        out_shape=jax.ShapeDtypeStruct((blocks, pairs // blocks // 2, 2 * cols), jnp.float32),
+        out_shape=jax.ShapeDtypeStruct((blocks, pairs // blocks, cols), jnp.float32),
         in_specs=[pl.BlockSpec(memory_space=pltpu.VMEM)] * 2,
         out_specs=pl.BlockSpec(memory_space=pltpu.VMEM),
         compiler_params=pltpu.CompilerParams(vmem_limit_bytes=room),
@@ -139,26 +138,27 @@
     lots = blocks_ref.shape[0]
     total = None
     for z in range(lots):
-        term = dot(ladder_ref[z], blocks_ref[z])
+        term = thin_dot(parted(ladder_ref[z]), parted(blocks_ref[z]), 0)
         total = term if z == 0 else total + term
-    halves, kept, norbs = 2, held.shape[0] // 2, out_ref.shape[2]
-    rows, cons = out_ref.shape[0] // halves, out_ref.shape[1] // kept
-    for s in range(halves * kept):
+    kinds = held.shape[0]
+    rows, _, norbs = out_ref.shape
+    lines = out_ref.shape[1] // kinds
+    for s in range(kinds):
         held[s] = total[:, s * lanes : (s + 1) * lanes]
-    for h in range(halves):
-        for i in range(kept):
-            for r in range(rows):
-                line = held[h * kept + i, pl.ds(r, cons, stride=rows), :]
-                out_ref[h * rows + r, pl.ds(i, cons, stride=kept), :] = line[:, :norbs]
-
-
-def finish(ladder, blocks, shape, kept):
+    for s in range(kinds):
+        for r in range(rows):
+            line = held[s, pl.ds(r, lines, stride=rows), :]
+            out_ref[r, pl.ds(s, lines, stride=kinds), :] = line[:, :norbs]
+
+
+def finish(ladder, blocks, shape):
+    kinds = blocks.shape[2] // lanes
     return pl.pallas_call(
         finish_kernel,
         out_shape=jax.ShapeDtypeStruct(shape, jnp.float32),
         in_specs=[pl.BlockSpec(memory_space=pltpu.VMEM)] * 2,
         out_specs=pl.BlockSpec(memory_space=pltpu.VMEM),
-        scratch_shapes=[pltpu.VMEM((2 * kept, ladder.shape[1], lanes), jnp.float32)],
+        scratch_shapes=[pltpu.VMEM((kinds, ladder.shape[1], lanes), jnp.float32)],
         compiler_params=pltpu.CompilerParams(vmem_limit_bytes=room),
     )(ladder, blocks)
 
@@ -167,9 +167,12 @@
     norbs = hole_hole.shape[0]
     naux = fit_con.shape[0]
     halves, lots = lax.axis_size("out_hi"), lax.axis_size("out_lo")
-    cons, occs = lax.axis_size("con"), lax.axis_size("occ")
+    lines, cores, occs = lax.axis_size("row"), lax.axis_size("core"), lax.axis_size("occ")
+    cons = lines * cores
     cols = amplitudes.shape[2]
     kept = norbs // (cons * occs)
+    _, pairs = fit_out.shape
+    rows = pairs // cons
     side = lax.axis_index("out_lo")
     dress = jnp.eye(norbs, dtype=jnp.float32) - hole_hole
 
@@ -177,37 +180,42 @@
     share = share.reshape(cons * occs, *share.shape[2:])
     parts = lax.all_to_all(share, plane, 0, 0, tiled=True)
     fitted = jnp.sum(parts, axis=0)
-    whole = lax.all_gather(fitted, "out_hi", axis=0)
-    other = lax.ppermute(fit_out, "out_lo", [(0, 1), (1, 0)])
-    factors = jnp.concatenate(
-        [jnp.where(side == 0, fit_out, other), jnp.where(side == 0, other, fit_out)], axis=1
+    whole = lax.all_gather(fitted, ("out_hi", "core"), axis=0)
+    index = jnp.arange(pairs)
+    origin = (index // rows % lines * cores + index // (rows * lines)) * rows + index % rows
+    chosen = (index[:, None] == origin[None]).astype(jnp.float32)
+    mine = jnp.dot(fit_out, chosen, precision=highest)
+    other = lax.ppermute(mine, "out_lo", [(0, 1), (1, 0)])
+    planes = [jnp.where(side == 0, mine, other), jnp.where(side == 0, other, mine)]
+    wide = pairs // cores
+    factors = jnp.stack(
+        [jnp.concatenate([p[:, c * wide : (c + 1) * wide] for p in planes], axis=1) for c in range(cores)]
     )
-    factors = jnp.broadcast_to(factors[None], (cons, *factors.shape))
-    factors = lax.all_to_all(factors, "con", 0, 0, tiled=True)
-    factors = factors.reshape(naux, lots * fit_out.shape[1])
-    ladder = contract(whole, factors, lots * cons)
+    factors = jnp.broadcast_to(factors[None], (lines, *factors.shape))
+    factors = lax.all_to_all(factors.reshape(cons, *factors.shape[2:]), con, 0, 0, tiled=True)
+    factors = factors.reshape(naux, lots * wide)
+    ladder = contract(whole, factors, lots * lines)
     ladder = lax.all_to_all(ladder, pair, 0, 0, tiled=True)
-    rows = fit_out.shape[1] // cons
-    ladder = ladder.reshape(lots, cons * rows // 2, lanes)
+    ladder = ladder.reshape(lots, lines * rows, lanes)
     orders = jnp.swapaxes(dress.T.reshape(halves, lots, cols, norbs), 0, 1)
     orders = jnp.pad(orders, ((0, 0), (0, 0), (0, 0), (0, lanes - norbs)))
-    orders = orders.reshape(lots, 1, halves, cols, 1, 1, 1, lanes)
-    same = jnp.eye(2, dtype=jnp.float32).reshape(1, 2, 1, 1, 1, 2, 1, 1)
+    orders = orders.reshape(lots, halves, 1, cols, 1, 1, 1, lanes)
+    same = jnp.eye(cores, dtype=jnp.float32).reshape(1, 1, cores, 1, 1, cores, 1, 1)
     kind = jnp.eye(kept, dtype=jnp.float32).reshape(1, 1, 1, 1, kept, 1, kept, 1)
-    blocks = (orders * same * kind).reshape(lots, lanes, 2 * kept * lanes)
-    return finish(ladder, blocks, (rows, cons * kept, norbs), kept)
+    blocks = (orders * same * kind).reshape(lots, lanes, cores * kept * lanes)
+    return finish(ladder, blocks, (rows, cons * kept, norbs))
 
 
 def solution(mesh):
-    lots = 2
+    lots, cores = 2, 2
     shape = dict(mesh.shape)
-    devices = mesh.devices.reshape(shape["out"] // lots, lots, shape["con"], shape["occ"])
-    finer = Mesh(devices, ("out_hi", "out_lo", "con", "occ"))
+    devices = mesh.devices.reshape(shape["out"] // lots, lots, shape["con"] // cores, cores, shape["occ"])
+    finer = Mesh(devices, ("out_hi", "out_lo", *con, "occ"))
     out = ("out_hi", "out_lo")
     return jax.shard_map(
         local,
         mesh=finer,
-        in_specs=(P("con", "occ", out), P("con", out), P(None, "con"), P()),
-        out_specs=P((*out, "con"), "occ", None),
+        in_specs=(P(con, "occ", out), P(con, out), P(None, con), P()),
+        out_specs=P((*out, *con), "occ", None),
         check_vma=False,
     )

time: 97.1 us -> 100 us (1.030)
  blocking collectives: 33.5 us -> 41.1 us
  starting transfers between devices: 38.5 us -> 32 us
  waiting for transfers between devices: 15.6 us -> 16.8 us
    all_gather x1, blocking collectives: 33.5 us -> 41.1 us  [local(): whole = lax.all_gather(fitted, ('out_hi', 'core'), axis=0)]
    all_to_all x1, starting transfers between devices: 13.7 us -> 7.19 us  [local(): ladder = lax.all_to_all(ladder, pair, 0, 0, tiled=True)]
    all_to_all x1, waiting for transfers between devices: 5.13 us -> 10.4 us  [local(): parts = lax.all_to_all(share, plane, 0, 0, tiled=True)]
    ppermute x1, waiting for transfers between devices: 3.37 us -> 0.01 us  [local(): other = lax.ppermute(mine, 'out_lo', [(0, 1), (1, 0)])]
    all_to_all x1, starting transfers between devices: 17.7 us -> 15.2 us  [local(): parts = lax.all_to_all(share, plane, 0, 0, tiled=True)]
    ppermute x1, starting transfers between devices: 1.92 us -> 4.36 us  [local(): other = lax.ppermute(mine, 'out_lo', [(0, 1), (1, 0)])]
  transfers between devices with their start and end apart: 4 -> 4, of which waited for: 3 -> 2; matrix products, arithmetic and copies ran while one was open for 1% -> 1% of each run, Pallas kernels for 0% -> 3%
where the time goes in v5:
time: 100 us; the launch traced here: 99.5 us
  blocking collectives  41.1 us (41%)
  starting transfers between devices  32 us (32%)
  waiting for transfers between devices  16.8 us (17%)
  Pallas kernels  5.87 us (6%)
  local copies, waits for them, and re-layouts  2.97 us (3%)
    all_gather x1, blocking collectives, local(): whole = lax.all_gather(fitted, ('out_hi', 'core'), axis=0)  41.1 us
    all_to_all x1, starting transfers between devices, local(): parts = lax.all_to_all(share, plane, 0, 0, tiled=True)  15.2 us
    all_to_all x1, waiting for transfers between devices, local(): parts = lax.all_to_all(share, plane, 0, 0, tiled=True)  10.4 us
    all_to_all x1, starting transfers between devices, local(): ladder = lax.all_to_all(ladder, pair, 0, 0, tiled=True)  7.19 us
    all_to_all x1, waiting for transfers between devices, local(): ladder = lax.all_to_all(ladder, pair, 0, 0, tiled=True)  6.46 us
    all_to_all x1, starting transfers between devices, local(): lax.all_to_all(factors.reshape(cons, *factors.shape[2:]), con, 0, 0, tile...  5.22 us
    ppermute x1, starting transfers between devices, local(): other = lax.ppermute(mine, 'out_lo', [(0, 1), (1, 0)])  4.36 us
    pallas_call x1, Pallas kernels, share_of(): pl.pallas_call(share_kernel, out_shape=jax.ShapeDtypeStruct((blocks // 2,...  3.18 us
  transfers between devices with their start and end apart: 4, of which 2 were waited for; matrix products, arithmetic and copies ran while one was open for 1% of the time, Pallas kernels for 3%

profile of v5, /device:TPU:1, one launch (start us, length us, event | category | flops | bytes accessed | tf_op | source)
XLA Modules:
  0.0 99.5 jit_solution(3553634087073625593)
XLA Ops:
  0.0 0.0 copy-start
  0.0 0.8 copy-done
  0.8 0.2 convolution_bitcast_fusion
  1.1 4.4 %collective-permute-start = (f32[64,256]{1,0:T(8,128)S(1)}, f32[64,256]{1,0:T(8,128)S(1)}, u32[]{:S(2)}, u32[]{:S(2)}) collective-permute-start(f32[64,256]{1,0:T(8,128)S(1)} %convolution_bitcast_fusion), channel_id=1, source_target_pairs={{0,32},{32,0},{1,33},{33,1},{2,34},{34,2},{3,35},{35,3},{4,36},{36... | collective-permute-start | bytes 196616 | tf_op jit(solution)/shard_map/ppermute | solution.py:188
  5.4 3.2 %shard_map.46 = f32[16,2,8,512]{3,2,1,0:T(8,128)} custom-call(f32[32,2,128]{2,1,0:T(2,128)} %bitcast.23, f32[1024,128]{1,0:T(8,128)} %lined_ref.1, f32[64,64]{1,0:T(8,128)} %hole_ref.1), custom_call_target="tpu_custom_call" | custom-call | tf_op jit(solution)/shard_map/pallas_call | solution.py:94
  8.6 15.2 %all-to-all-start = ((f32[32,8,512]{2,1,0:T(8,128)}), f32[32,8,512]{2,1,0:T(8,128)S(1)}, u32[]{:S(2)}, u32[]{:S(2)}) async-start(f32[32,8,512]{2,1,0:T(8,128)} %bitcast.21), calls=%async_computation | async-start | bytes 1048576 | tf_op jit(solution)/shard_map/all_to_all | solution.py:181
  23.9 0.0 collective-permute-done
  24.0 10.4 %all-to-all-done = f32[32,8,512]{2,1,0:T(8,128)S(1)} async-done(((f32[32,8,512]{2,1,0:T(8,128)}), f32[32,8,512]{2,1,0:T(8,128)S(1)}, u32[]{:S(2)}, u32[]{:S(2)}) %all-to-all-start) | async-done | bytes 524320 | tf_op jit(solution)/shard_map/all_to_all | solution.py:181
  34.4 1.1 %broadcast_in_dim.2 = f32[8,2,64,256]{3,2,1,0:T(8,128)} broadcast(f32[2,64,256]{2,1,0:T(8,128)S(1)} %pad_maximum_fusion), dimensions={1,2,3} | broadcast | bytes 1179648 | tf_op jit(solution)/shard_map/broadcast_in_dim | solution.py:194
  35.4 5.2 %all-to-all-start.1 = ((f32[16,64,256]{2,1,0:T(8,128)}), f32[16,64,256]{2,1,0:T(8,128)S(1)}, u32[]{:S(2)}, u32[]{:S(2)}) async-start(f32[16,64,256]{2,1,0:T(8,128)} %bitcast.6), calls=%async_computation.1 | async-start | bytes 2097152 | tf_op jit(solution)/shard_map/all_to_all | solution.py:195
  40.7 41.1 %all-gather = f32[256,512]{1,0:T(8,128)S(1)} all-gather(f32[8,512]{1,0:T(8,128)S(1)} %reduce_sum.9), channel_id=2, replica_groups=mesh['out_hi'=16,'out_lo'=2,'row'=8,'core'=2,'occ'=2] {'out_hi','core'}, dimensions={0}, use_global_device_ids=true | all-gather | bytes 540672 | tf_op jit(solution)/shard_map/all_gather | solution.py:183
  81.8 0.0 all-to-all-done.1
  81.8 1.4 %shard_map.47 = f32[16,16,128]{2,1,0:T(8,128)} custom-call(f32[32,8,512]{2,1,0:T(8,128)S(1)} %bitcast.19, f32[1024,256]{1,0:T(8,128)S(1)} %bitcast.18), custom_call_target="tpu_custom_call" | custom-call | tf_op jit(solution)/shard_map/pallas_call | solution.py:128
  83.2 0.0 copy-start.1
  83.2 7.2 %all-to-all-start.2 = ((f32[16,16,128]{2,1,0:T(8,128)}), f32[16,16,128]{2,1,0:T(8,128)S(1)}, u32[]{:S(2)}, u32[]{:S(2)}) async-start(f32[16,16,128]{2,1,0:T(8,128)} %shard_map.47), calls=%async_computation.2 | async-start | bytes 262144 | tf_op jit(solution)/shard_map/all_to_all | solution.py:198
  90.4 0.0 copy-done.1
  90.4 0.1 copy.6
  90.5 0.1 broadcast_multiply_fusion.1
  90.6 0.2 mul.62
  90.8 0.4 mul.63
  91.2 0.2 mul.64
  91.4 0.2 mul.65
  91.6 0.1 broadcast_multiply_fusion.blocks_ref
  91.7 6.5 %all-to-all-done.2 = f32[16,16,128]{2,1,0:T(8,128)S(1)} async-done(((f32[16,16,128]{2,1,0:T(8,128)}), f32[16,16,128]{2,1,0:T(8,128)S(1)}, u32[]{:S(2)}, u32[]{:S(2)}) %all-to-all-start.2) | async-done | bytes 131104 | tf_op jit(solution)/shard_map/all_to_all | solution.py:198
  98.1 1.3 %shard_map.48 = f32[16,32,64]{2,1,0:T(8,128)} custom-call(f32[2,128,128]{2,1,0:T(8,128)S(1)} %bitcast.20, f32[2,128,512]{2,1,0:T(8,128)S(1)} %broadcast_multiply_fusion.blocks_ref), custom_call_target="tpu_custom_call" | custom-call | tf_op jit(solution)/shard_map/pallas_call | solution.py:156
  (11 shorter events, 0.2 us)
Async XLA Ops:
  0.0 0.8 copy-start
  1.1 22.8 %collective-permute-start = (f32[64,256]{1,0:T(8,128)S(1)}, f32[64,256]{1,0:T(8,128)S(1)}, u32[]{:S(2)}, u32[]{:S(2)}) collective-permute-start(f32[64,256]{1,0:T(8,128)S(1)} %convolution_bitcast_fusion), channel_id=1, source_target_pairs={{0,32},{32,0},{1,33},{33,1},{2,34},{34,2},{3,35},{35,3},{4,36},{36... | collective-permute-start | bytes 196616 | tf_op jit(solution)/shard_map/ppermute | solution.py:188
  8.6 25.7 %all-to-all-start = ((f32[32,8,512]{2,1,0:T(8,128)}), f32[32,8,512]{2,1,0:T(8,128)S(1)}, u32[]{:S(2)}, u32[]{:S(2)}) async-start(f32[32,8,512]{2,1,0:T(8,128)} %bitcast.21), calls=%async_computation | async-start | bytes 1048576 | tf_op jit(solution)/shard_map/all_to_all | solution.py:181
  35.4 46.4 %all-to-all-start.1 = ((f32[16,64,256]{2,1,0:T(8,128)}), f32[16,64,256]{2,1,0:T(8,128)S(1)}, u32[]{:S(2)}, u32[]{:S(2)}) async-start(f32[16,64,256]{2,1,0:T(8,128)} %bitcast.6), calls=%async_computation.1 | async-start | bytes 2097152 | tf_op jit(solution)/shard_map/all_to_all | solution.py:195
  83.2 7.2 %copy-start.1 = (f32[64,64]{1,0:T(8,128)S(1)}, f32[64,64]{1,0:T(8,128)}, u32[]{:S(2)}) copy-start(f32[64,64]{1,0:T(8,128)} %hole_ref.1) | copy-start | bytes 49156
  83.2 15.0 %all-to-all-start.2 = ((f32[16,16,128]{2,1,0:T(8,128)}), f32[16,16,128]{2,1,0:T(8,128)S(1)}, u32[]{:S(2)}, u32[]{:S(2)}) async-start(f32[16,16,128]{2,1,0:T(8,128)} %shard_map.47), calls=%async_computation.2 | async-start | bytes 262144 | tf_op jit(solution)/shard_map/all_to_all | solution.py:198

commit v6 on v5

--- a/solution.py
+++ b/solution.py
@@ -42,68 +42,80 @@
     return lax.broadcasted_iota(jnp.int32, shape, len(shape) - 2) < shape[-2] // 2
 
 
-def share_kernel(given_ref, lined_ref, hole_ref, share_ref, given, lined, hole, padded, arrived):
-    own, cols, _ = given.shape
+def share_kernel(given_ref, lined_ref, hole_ref, share_ref, given, lined, hole, padded, share, arrived, left):
+    own, cols, width = given.shape
     norbs = hole.shape[0]
-    blocks = 2 * share_ref.shape[0]
+    steps, _, chunk, _ = lined.shape
+    blocks = 2 * share.shape[0]
     occs = norbs // own
     kept = norbs // blocks
-    half = lined.shape[0] // 2
     copies = [
         pltpu.make_async_copy(given_ref, given, arrived.at[0]),
         pltpu.make_async_copy(hole_ref, hole, arrived.at[1]),
     ]
-    for c in range(2):
-        rows = pl.ds(c * half, half)
-        copies.append(pltpu.make_async_copy(lined_ref.at[rows, :], lined.at[rows, :], arrived.at[2 + c]))
+    for q in range(steps):
+        copies.append(pltpu.make_async_copy(lined_ref.at[:, q], lined.at[q], arrived.at[2 + q]))
     for copy in copies:
         copy.start()
     padded[...] = jnp.zeros_like(padded)
-    place = lax.broadcasted_iota(jnp.int32, (blocks * cols * kept, norbs), 0)
+    square = (blocks * cols * kept, cols * norbs)
+    place = lax.broadcasted_iota(jnp.int32, square, 0)
+    index = lax.broadcasted_iota(jnp.int32, square, 1)
     device, inner = place // (cols * kept), place % (cols * kept)
-    wanted = (device % occs) * own + (device // occs) * kept + inner % kept
-    index = lax.broadcasted_iota(jnp.int32, (blocks * cols * kept, norbs), 1)
+    wanted = (device % occs) * own + (device // occs) * kept + inner % kept + inner // kept * norbs
+    chosen = jnp.where(wanted == index, 1.0, 0.0).astype(jnp.bfloat16)
     square = (norbs, norbs)
     unit = lax.broadcasted_iota(jnp.int32, square, 0) == lax.broadcasted_iota(jnp.int32, square, 1)
     first = pl.multiple_of(lax.axis_index("occ") * own, own)
     copies[0].wait()
+    for j in range(cols):
+        padded[pl.ds(first, own), j * width : (j + 1) * width] = given[:, j, :]
     copies[1].wait()
-    dress = jnp.where(unit, 1.0, 0.0) - hole[...]
-    total = None
-    for j in range(cols):
-        padded[j, pl.ds(first, own), :] = given[:, j, :]
-        dressed = dot(dress, padded[j])
-        chosen = jnp.where((wanted == index) & (inner // kept == j), 1.0, 0.0)
-        term = dot(chosen, dressed)
-        total = term if j == 0 else total + term
-    total = parted(total)
-    found = []
-    for c in range(2):
-        copies[2 + c].wait()
-        term = thin_dot(total, parted(lined[c * half : (c + 1) * half, :]), 1)
-        found.append(term.reshape(blocks // 2, 2 * cols * kept, half))
-    lower = lower_rows(found[0].shape)
-    turned = [pltpu.roll(term, cols * kept, 1) for term in found]
-    share_ref[:, 0] = jnp.where(lower, found[0], turned[1])
-    share_ref[:, 1] = jnp.where(lower, turned[0], found[1])
+    dressed = dot(jnp.where(unit, 1.0, 0.0) - hole[...], padded[...])
+    dressed = jnp.concatenate([dressed[:, j * width : (j + 1) * width] for j in range(cols)], axis=0)
+    picked = narrow(chosen, jnp.concatenate(parted(dressed), axis=1), 0)
+    total = tuple(picked[:, k * width : (k + 1) * width].astype(jnp.bfloat16) for k in range(3))
+    sends = []
+    for q in range(steps):
+        copies[2 + q].wait()
+        term = thin_dot(total, parted(lined[q].reshape(2 * chunk, width)), 1)
+        found = [
+            term[:, c * chunk : (c + 1) * chunk].reshape(blocks // 2, 2 * cols * kept, chunk) for c in range(2)
+        ]
+        lower = lower_rows(found[0].shape)
+        turned = [pltpu.roll(part, cols * kept, 1) for part in found]
+        lot = pl.ds(q * chunk, chunk)
+        share[:, 0, :, q * chunk : (q + 1) * chunk] = jnp.where(lower, found[0], turned[1])
+        share[:, 1, :, q * chunk : (q + 1) * chunk] = jnp.where(lower, turned[0], found[1])
+        sends.append(
+            pltpu.make_async_copy(share.at[:, :, :, lot], share_ref.at[:, :, :, lot], left.at[q])
+        )
+        sends[-1].start()
+    for send in sends:
+        send.wait()
 
 
 def share_of(given, lined, hole, blocks):
-    naux = lined.shape[0]
+    steps = 4
+    naux, width = lined.shape
     rows = 2 * given.shape[1] * hole.shape[0] // blocks
+    shape = (blocks // 2, 2, rows, naux // 2)
+    chunk = naux // 2 // steps
     return pl.pallas_call(
         share_kernel,
-        out_shape=jax.ShapeDtypeStruct((blocks // 2, 2, rows, naux // 2), jnp.float32),
+        out_shape=jax.ShapeDtypeStruct(shape, jnp.float32),
         in_specs=[pl.BlockSpec(memory_space=pl.ANY)] * 3,
-        out_specs=pl.BlockSpec(memory_space=pltpu.VMEM),
+        out_specs=pl.BlockSpec(memory_space=pl.ANY),
         scratch_shapes=[
             pltpu.VMEM(given.shape, jnp.float32),
-            pltpu.VMEM(lined.shape, jnp.float32),
+            pltpu.VMEM((steps, 2, chunk, width), jnp.float32),
             pltpu.VMEM(hole.shape, jnp.float32),
-            pltpu.VMEM((given.shape[1], hole.shape[0], given.shape[2]), jnp.float32),
-            pltpu.SemaphoreType.DMA((4,)),
+            pltpu.VMEM((hole.shape[0], given.shape[1] * given.shape[2]), jnp.float32),
+            pltpu.VMEM(shape, jnp.float32),
+            pltpu.SemaphoreType.DMA((2 + steps,)),
+            pltpu.SemaphoreType.DMA((steps,)),
         ],
-    )(given, lined, hole)
+    )(given, lined.reshape(2, steps, chunk, width), hole)
 
 
 def contract_kernel(fitted_ref, factors_ref, ladder_ref):
@@ -134,11 +146,26 @@
     )(fitted, factors)
 
 
+def pieces_kernel(blocks_ref, pieces_ref):
+    for k, piece in enumerate(parted(blocks_ref[...])):
+        pieces_ref[k] = piece
+
+
+def pieces_of(blocks):
+    return pl.pallas_call(
+        pieces_kernel,
+        out_shape=jax.ShapeDtypeStruct((3, *blocks.shape), jnp.bfloat16),
+        in_specs=[pl.BlockSpec(memory_space=pltpu.VMEM)],
+        out_specs=pl.BlockSpec(memory_space=pltpu.VMEM),
+        compiler_params=pltpu.CompilerParams(vmem_limit_bytes=room),
+    )(blocks)
+
+
 def finish_kernel(ladder_ref, blocks_ref, out_ref, held):
-    lots = blocks_ref.shape[0]
+    lots = blocks_ref.shape[1]
     total = None
     for z in range(lots):
-        term = thin_dot(parted(ladder_ref[z]), parted(blocks_ref[z]), 0)
+        term = thin_dot(parted(ladder_ref[z]), tuple(blocks_ref[k, z] for k in range(3)), 0)
         total = term if z == 0 else total + term
     kinds = held.shape[0]
     rows, _, norbs = out_ref.shape
@@ -152,7 +179,7 @@
 
 
 def finish(ladder, blocks, shape):
-    kinds = blocks.shape[2] // lanes
+    kinds = blocks.shape[3] // lanes
     return pl.pallas_call(
         finish_kernel,
         out_shape=jax.ShapeDtypeStruct(shape, jnp.float32),
@@ -203,6 +230,7 @@
     same = jnp.eye(cores, dtype=jnp.float32).reshape(1, 1, cores, 1, 1, cores, 1, 1)
     kind = jnp.eye(kept, dtype=jnp.float32).reshape(1, 1, 1, 1, kept, 1, kept, 1)
     blocks = (orders * same * kind).reshape(lots, lanes, cores * kept * lanes)
+    blocks = pieces_of(blocks)
     return finish(ladder, blocks, (rows, cons * kept, norbs))
 
 

time: 100 us -> 100 us (level)
    pallas_call x1 -> x2, Pallas kernels: 3.18 us -> 3.52 us  [the longest x1 3.37 us: share_of(): pl.pallas_call(share_kernel, out_shape=jax.ShapeDtypeStruct(shape, jnp.fl...]
  transfers between devices with their start and end apart: 4 -> 4, of which waited for: 2 -> 2; matrix products, arithmetic and copies ran while one was open for 1% -> 1% of each run, Pallas kernels for 3% -> 4%
where the time goes in v6:
time: 100 us; the launch traced here: 99.7 us
  blocking collectives  41.1 us (41%)
  starting transfers between devices  32 us (32%)
  waiting for transfers between devices  16.7 us (17%)
  Pallas kernels  6.2 us (6%)
  local copies, waits for them, and re-layouts  2.97 us (3%)
    all_gather x1, blocking collectives, local(): whole = lax.all_gather(fitted, ('out_hi', 'core'), axis=0)  41.1 us
    all_to_all x1, starting transfers between devices, local(): parts = lax.all_to_all(share, plane, 0, 0, tiled=True)  15.2 us
    all_to_all x1, waiting for transfers between devices, local(): parts = lax.all_to_all(share, plane, 0, 0, tiled=True)  10.4 us
    all_to_all x1, starting transfers between devices, local(): ladder = lax.all_to_all(ladder, pair, 0, 0, tiled=True)  7.19 us
    all_to_all x1, waiting for transfers between devices, local(): ladder = lax.all_to_all(ladder, pair, 0, 0, tiled=True)  6.3 us
    all_to_all x1, starting transfers between devices, local(): lax.all_to_all(factors.reshape(cons, *factors.shape[2:]), con, 0, 0, tile...  5.22 us
    ppermute x1, starting transfers between devices, local(): other = lax.ppermute(mine, 'out_lo', [(0, 1), (1, 0)])  4.36 us
    pallas_call x1, Pallas kernels, share_of(): pl.pallas_call(share_kernel, out_shape=jax.ShapeDtypeStruct(shape, jnp.fl...  3.37 us
  transfers between devices with their start and end apart: 4, of which 2 were waited for; matrix products, arithmetic and copies ran while one was open for 1% of the time, Pallas kernels for 4%

profile of v6, /device:TPU:1, one launch (start us, length us, event | category | flops | bytes accessed | tf_op | source)
XLA Modules:
  0.0 99.7 jit_solution(5696140544457398355)
XLA Ops:
  0.0 0.0 copy-start
  0.0 0.8 copy-done
  0.8 0.2 convolution_bitcast_fusion
  1.1 4.4 %collective-permute-start = (f32[64,256]{1,0:T(8,128)S(1)}, f32[64,256]{1,0:T(8,128)S(1)}, u32[]{:S(2)}, u32[]{:S(2)}) collective-permute-start(f32[64,256]{1,0:T(8,128)S(1)} %convolution_bitcast_fusion), channel_id=1, source_target_pairs={{0,32},{32,0},{1,33},{33,1},{2,34},{34,2},{3,35},{35,3},{4,36},{36... | collective-permute-start | bytes 196616 | tf_op jit(solution)/shard_map/ppermute | solution.py:215
  5.4 3.4 %shard_map.46 = f32[16,2,8,512]{3,2,1,0:T(8,128)} custom-call(f32[32,2,128]{2,1,0:T(2,128)} %bitcast.25, f32[2,4,128,128]{3,2,1,0:T(8,128)} %bitcast.23, f32[64,64]{1,0:T(8,128)} %hole_ref.1), custom_call_target="tpu_custom_call" | custom-call | tf_op jit(solution)/shard_map/pallas_call | solution.py:104
  8.8 15.2 %all-to-all-start = ((f32[32,8,512]{2,1,0:T(8,128)}), f32[32,8,512]{2,1,0:T(8,128)S(1)}, u32[]{:S(2)}, u32[]{:S(2)}) async-start(f32[32,8,512]{2,1,0:T(8,128)} %bitcast.22), calls=%async_computation | async-start | bytes 1048576 | tf_op jit(solution)/shard_map/all_to_all | solution.py:208
  24.1 0.0 collective-permute-done
  24.2 10.4 %all-to-all-done = f32[32,8,512]{2,1,0:T(8,128)S(1)} async-done(((f32[32,8,512]{2,1,0:T(8,128)}), f32[32,8,512]{2,1,0:T(8,128)S(1)}, u32[]{:S(2)}, u32[]{:S(2)}) %all-to-all-start) | async-done | bytes 524320 | tf_op jit(solution)/shard_map/all_to_all | solution.py:208
  34.5 1.1 %broadcast_in_dim.2 = f32[8,2,64,256]{3,2,1,0:T(8,128)} broadcast(f32[2,64,256]{2,1,0:T(8,128)S(1)} %pad_maximum_fusion), dimensions={1,2,3} | broadcast | bytes 1179648 | tf_op jit(solution)/shard_map/broadcast_in_dim | solution.py:221
  35.6 5.2 %all-to-all-start.1 = ((f32[16,64,256]{2,1,0:T(8,128)}), f32[16,64,256]{2,1,0:T(8,128)S(1)}, u32[]{:S(2)}, u32[]{:S(2)}) async-start(f32[16,64,256]{2,1,0:T(8,128)} %bitcast.7), calls=%async_computation.1 | async-start | bytes 2097152 | tf_op jit(solution)/shard_map/all_to_all | solution.py:222
  40.9 41.1 %all-gather = f32[256,512]{1,0:T(8,128)S(1)} all-gather(f32[8,512]{1,0:T(8,128)S(1)} %reduce_sum.9), channel_id=2, replica_groups=mesh['out_hi'=16,'out_lo'=2,'row'=8,'core'=2,'occ'=2] {'out_hi','core'}, dimensions={0}, use_global_device_ids=true | all-gather | bytes 540672 | tf_op jit(solution)/shard_map/all_gather | solution.py:210
  82.0 0.0 all-to-all-done.1
  82.0 1.3 %shard_map.47 = f32[16,16,128]{2,1,0:T(8,128)} custom-call(f32[32,8,512]{2,1,0:T(8,128)S(1)} %bitcast.20, f32[1024,256]{1,0:T(8,128)S(1)} %bitcast.19), custom_call_target="tpu_custom_call" | custom-call | tf_op jit(solution)/shard_map/pallas_call | solution.py:140
  83.3 0.0 copy-start.1
  83.3 7.2 %all-to-all-start.2 = ((f32[16,16,128]{2,1,0:T(8,128)}), f32[16,16,128]{2,1,0:T(8,128)S(1)}, u32[]{:S(2)}, u32[]{:S(2)}) async-start(f32[16,16,128]{2,1,0:T(8,128)} %shard_map.47), calls=%async_computation.2 | async-start | bytes 262144 | tf_op jit(solution)/shard_map/all_to_all | solution.py:225
  90.5 0.0 copy-done.1
  90.6 0.1 copy.6
  90.7 0.1 broadcast_multiply_fusion.1
  90.8 0.2 mul.62
  91.0 0.4 mul.63
  91.4 0.2 mul.64
  91.6 0.2 mul.65
  91.8 0.1 broadcast_multiply_fusion.blocks_ref
  91.9 0.1 shard_map.48.blocks_ref
  92.0 6.3 %all-to-all-done.2 = f32[16,16,128]{2,1,0:T(8,128)S(1)} async-done(((f32[16,16,128]{2,1,0:T(8,128)}), f32[16,16,128]{2,1,0:T(8,128)S(1)}, u32[]{:S(2)}, u32[]{:S(2)}) %all-to-all-start.2) | async-done | bytes 131104 | tf_op jit(solution)/shard_map/all_to_all | solution.py:225
  98.3 1.3 %shard_map.49 = f32[16,32,64]{2,1,0:T(8,128)} custom-call(f32[2,128,128]{2,1,0:T(8,128)S(1)} %bitcast.21, bf16[3,2,128,512]{3,2,1,0:T(8,128)(2,1)S(1)} %shard_map.48.blocks_ref), custom_call_target="tpu_custom_call" | custom-call | tf_op jit(solution)/shard_map/pallas_call | solution.py:183
  (11 shorter events, 0.2 us)
Async XLA Ops:
  0.0 0.8 copy-start
  1.1 23.0 %collective-permute-start = (f32[64,256]{1,0:T(8,128)S(1)}, f32[64,256]{1,0:T(8,128)S(1)}, u32[]{:S(2)}, u32[]{:S(2)}) collective-permute-start(f32[64,256]{1,0:T(8,128)S(1)} %convolution_bitcast_fusion), channel_id=1, source_target_pairs={{0,32},{32,0},{1,33},{33,1},{2,34},{34,2},{3,35},{35,3},{4,36},{36... | collective-permute-start | bytes 196616 | tf_op jit(solution)/shard_map/ppermute | solution.py:215
  8.8 25.7 %all-to-all-start = ((f32[32,8,512]{2,1,0:T(8,128)}), f32[32,8,512]{2,1,0:T(8,128)S(1)}, u32[]{:S(2)}, u32[]{:S(2)}) async-start(f32[32,8,512]{2,1,0:T(8,128)} %bitcast.22), calls=%async_computation | async-start | bytes 1048576 | tf_op jit(solution)/shard_map/all_to_all | solution.py:208
  35.6 46.4 %all-to-all-start.1 = ((f32[16,64,256]{2,1,0:T(8,128)}), f32[16,64,256]{2,1,0:T(8,128)S(1)}, u32[]{:S(2)}, u32[]{:S(2)}) async-start(f32[16,64,256]{2,1,0:T(8,128)} %bitcast.7), calls=%async_computation.1 | async-start | bytes 2097152 | tf_op jit(solution)/shard_map/all_to_all | solution.py:222
  83.3 7.2 %copy-start.1 = (f32[64,64]{1,0:T(8,128)S(1)}, f32[64,64]{1,0:T(8,128)}, u32[]{:S(2)}) copy-start(f32[64,64]{1,0:T(8,128)} %hole_ref.1) | copy-start | bytes 49156
  83.3 15.0 %all-to-all-start.2 = ((f32[16,16,128]{2,1,0:T(8,128)}), f32[16,16,128]{2,1,0:T(8,128)S(1)}, u32[]{:S(2)}, u32[]{:S(2)}) async-start(f32[16,16,128]{2,1,0:T(8,128)} %shard_map.47), calls=%async_computation.2 | async-start | bytes 262144 | tf_op jit(solution)/shard_map/all_to_all | solution.py:225

commit v7 on v6

--- a/solution.py
+++ b/solution.py
@@ -193,21 +193,24 @@
 def local(amplitudes, fit_out, fit_con, hole_hole):
     norbs = hole_hole.shape[0]
     naux = fit_con.shape[0]
-    halves, lots = lax.axis_size("out_hi"), lax.axis_size("out_lo")
+    highs, mids, lots = lax.axis_size("out_hi"), lax.axis_size("out_mid"), lax.axis_size("out_lo")
     lines, cores, occs = lax.axis_size("row"), lax.axis_size("core"), lax.axis_size("occ")
     cons = lines * cores
     cols = amplitudes.shape[2]
     kept = norbs // (cons * occs)
     _, pairs = fit_out.shape
     rows = pairs // cons
-    side = lax.axis_index("out_lo")
+    mid, side = lax.axis_index("out_mid"), lax.axis_index("out_lo")
     dress = jnp.eye(norbs, dtype=jnp.float32) - hole_hole
 
     share = share_of(jnp.transpose(amplitudes, (1, 2, 0)), fit_con, hole_hole, cons * occs)
     share = share.reshape(cons * occs, *share.shape[2:])
     parts = lax.all_to_all(share, plane, 0, 0, tiled=True)
     fitted = jnp.sum(parts, axis=0)
-    whole = lax.all_gather(fitted, ("out_hi", "core"), axis=0)
+    beyond = lax.ppermute(fitted, "out_mid", [(0, 1), (1, 0)])
+    both = jnp.stack([jnp.where(mid == 0, fitted, beyond), jnp.where(mid == 0, beyond, fitted)])
+    whole = lax.all_gather(both, ("out_hi", "core"), axis=0)
+    whole = whole.reshape(-1, *whole.shape[2:])
     index = jnp.arange(pairs)
     origin = (index // rows % lines * cores + index // (rows * lines)) * rows + index % rows
     chosen = (index[:, None] == origin[None]).astype(jnp.float32)
@@ -224,22 +227,21 @@
     ladder = contract(whole, factors, lots * lines)
     ladder = lax.all_to_all(ladder, pair, 0, 0, tiled=True)
     ladder = ladder.reshape(lots, lines * rows, lanes)
-    orders = jnp.swapaxes(dress.T.reshape(halves, lots, cols, norbs), 0, 1)
-    orders = jnp.pad(orders, ((0, 0), (0, 0), (0, 0), (0, lanes - norbs)))
-    orders = orders.reshape(lots, halves, 1, cols, 1, 1, 1, lanes)
-    same = jnp.eye(cores, dtype=jnp.float32).reshape(1, 1, cores, 1, 1, cores, 1, 1)
-    kind = jnp.eye(kept, dtype=jnp.float32).reshape(1, 1, 1, 1, kept, 1, kept, 1)
+    orders = jnp.transpose(dress.T.reshape(highs, mids, lots, cols, norbs), (2, 0, 1, 3, 4))
+    orders = jnp.pad(orders, ((0, 0),) * 4 + ((0, lanes - norbs),))
+    orders = orders.reshape(lots, highs, 1, mids, cols, 1, 1, 1, lanes)
+    same = jnp.eye(cores, dtype=jnp.float32).reshape(1, 1, cores, 1, 1, 1, cores, 1, 1)
+    kind = jnp.eye(kept, dtype=jnp.float32).reshape(1, 1, 1, 1, 1, kept, 1, kept, 1)
     blocks = (orders * same * kind).reshape(lots, lanes, cores * kept * lanes)
     blocks = pieces_of(blocks)
     return finish(ladder, blocks, (rows, cons * kept, norbs))
 
 
 def solution(mesh):
-    lots, cores = 2, 2
     shape = dict(mesh.shape)
-    devices = mesh.devices.reshape(shape["out"] // lots, lots, shape["con"] // cores, cores, shape["occ"])
-    finer = Mesh(devices, ("out_hi", "out_lo", *con, "occ"))
-    out = ("out_hi", "out_lo")
+    out = ("out_hi", "out_mid", "out_lo")
+    sizes = (shape["out"] // 4, 2, 2, shape["con"] // 2, 2, shape["occ"])
+    finer = Mesh(mesh.devices.reshape(sizes), (*out, *con, "occ"))
     return jax.shard_map(
         local,
         mesh=finer,

time: 100 us -> 99.7 us (level)
  blocking collectives: 41.1 us -> 34.4 us
  waiting for transfers between devices: 16.7 us -> 20.4 us
  starting transfers between devices: 32 us -> 34.4 us
    all_gather x1, blocking collectives: 41.1 us -> 34.4 us  [local(): whole = lax.all_gather(both, ('out_hi', 'core'), axis=0)]
    ppermute x0 -> x1, waiting for transfers between devices: none -> 3.74 us  [local(): beyond = lax.ppermute(fitted, 'out_mid', [(0, 1), (1, 0)])]
    ppermute x0 -> x1, starting transfers between devices: none -> 1.92 us  [local(): beyond = lax.ppermute(fitted, 'out_mid', [(0, 1), (1, 0)])]
  transfers between devices with their start and end apart: 4 -> 5, of which waited for: 2 -> 3; matrix products, arithmetic and copies ran while one was open for 1% -> 1% of each run, Pallas kernels for 4% -> 4%
where the time goes in v7:
time: 99.7 us; the launch traced here: 99.1 us
  starting transfers between devices  34.4 us (35%)
  blocking collectives  34.4 us (35%)
  waiting for transfers between devices  20.4 us (20%)
  Pallas kernels  6.2 us (6%)
  local copies, waits for them, and re-layouts  2.98 us (3%)
    all_gather x1, blocking collectives, local(): whole = lax.all_gather(both, ('out_hi', 'core'), axis=0)  34.4 us
    all_to_all x1, starting transfers between devices, local(): parts = lax.all_to_all(share, plane, 0, 0, tiled=True)  15.2 us
    all_to_all x1, waiting for transfers between devices, local(): parts = lax.all_to_all(share, plane, 0, 0, tiled=True)  10.4 us
    all_to_all x1, starting transfers between devices, local(): ladder = lax.all_to_all(ladder, pair, 0, 0, tiled=True)  7.69 us
    all_to_all x1, waiting for transfers between devices, local(): ladder = lax.all_to_all(ladder, pair, 0, 0, tiled=True)  6.3 us
    all_to_all x1, starting transfers between devices, local(): lax.all_to_all(factors.reshape(cons, *factors.shape[2:]), con, 0, 0, tile...  5.22 us
    ppermute x1, starting transfers between devices, local(): other = lax.ppermute(mine, 'out_lo', [(0, 1), (1, 0)])  4.36 us
    ppermute x1, waiting for transfers between devices, local(): beyond = lax.ppermute(fitted, 'out_mid', [(0, 1), (1, 0)])  3.74 us
  transfers between devices with their start and end apart: 5, of which 3 were waited for; matrix products, arithmetic and copies ran while one was open for 1% of the time, Pallas kernels for 4%

profile of v7, /device:TPU:1, one launch (start us, length us, event | category | flops | bytes accessed | tf_op | source)
XLA Modules:
  0.0 99.1 jit_solution(965380138373595085)
XLA Ops:
  0.0 0.0 copy-start
  0.0 0.8 copy-done
  0.8 0.2 convolution_bitcast_fusion
  1.1 4.4 %collective-permute-start.1 = (f32[64,256]{1,0:T(8,128)S(1)}, f32[64,256]{1,0:T(8,128)S(1)}, u32[]{:S(2)}, u32[]{:S(2)}) collective-permute-start(f32[64,256]{1,0:T(8,128)S(1)} %convolution_bitcast_fusion), channel_id=1, source_target_pairs={{0,32},{32,0},{1,33},{33,1},{2,34},{34,2},{3,35},{35,3},{4,36},{36... | collective-permute-start | bytes 196616 | tf_op jit(solution)/shard_map/ppermute | solution.py:218
  5.4 3.4 %shard_map.46 = f32[16,2,8,512]{3,2,1,0:T(8,128)} custom-call(f32[32,2,128]{2,1,0:T(2,128)} %bitcast.27, f32[2,4,128,128]{3,2,1,0:T(8,128)} %bitcast.25, f32[64,64]{1,0:T(8,128)} %hole_ref.1), custom_call_target="tpu_custom_call" | custom-call | tf_op jit(solution)/shard_map/pallas_call | solution.py:104
  8.8 15.2 %all-to-all-start = ((f32[32,8,512]{2,1,0:T(8,128)}), f32[32,8,512]{2,1,0:T(8,128)S(1)}, u32[]{:S(2)}, u32[]{:S(2)}) async-start(f32[32,8,512]{2,1,0:T(8,128)} %bitcast.24), calls=%async_computation | async-start | bytes 1048576 | tf_op jit(solution)/shard_map/all_to_all | solution.py:208
  24.1 0.0 collective-permute-done.1
  24.2 10.4 %all-to-all-done = f32[32,8,512]{2,1,0:T(8,128)S(1)} async-done(((f32[32,8,512]{2,1,0:T(8,128)}), f32[32,8,512]{2,1,0:T(8,128)S(1)}, u32[]{:S(2)}, u32[]{:S(2)}) %all-to-all-start) | async-done | bytes 524320 | tf_op jit(solution)/shard_map/all_to_all | solution.py:208
  34.5 1.1 %broadcast_in_dim.2 = f32[8,2,64,256]{3,2,1,0:T(8,128)} broadcast(f32[2,64,256]{2,1,0:T(8,128)S(1)} %pad_maximum_fusion), dimensions={1,2,3} | broadcast | bytes 1179648 | tf_op jit(solution)/shard_map/broadcast_in_dim | solution.py:224
  35.6 5.2 %all-to-all-start.1 = ((f32[16,64,256]{2,1,0:T(8,128)}), f32[16,64,256]{2,1,0:T(8,128)S(1)}, u32[]{:S(2)}, u32[]{:S(2)}) async-start(f32[16,64,256]{2,1,0:T(8,128)} %bitcast.8), calls=%async_computation.1 | async-start | bytes 2097152 | tf_op jit(solution)/shard_map/all_to_all | solution.py:225
  40.9 1.9 %collective-permute-start = (f32[8,512]{1,0:T(8,128)S(1)}, f32[8,512]{1,0:T(8,128)S(1)}, u32[]{:S(2)}, u32[]{:S(2)}) collective-permute-start(f32[8,512]{1,0:T(8,128)S(1)} %reduce_sum.9), channel_id=1, source_target_pairs={{0,64},{64,0},{1,65},{65,1},{2,66},{66,2},{3,67},{67,3},{4,68},{68... | collective-permute-start | bytes 49160 | tf_op jit(solution)/shard_map/ppermute | solution.py:210
  42.8 3.7 %collective-permute-done = f32[8,512]{1,0:T(8,128)S(1)} collective-permute-done((f32[8,512]{1,0:T(8,128)S(1)}, f32[8,512]{1,0:T(8,128)S(1)}, u32[]{:S(2)}, u32[]{:S(2)}) %collective-permute-start) | collective-permute-done | bytes 16416 | tf_op jit(solution)/shard_map/ppermute | solution.py:210
  46.6 34.4 %all-gather.fitted_ref = f32[32,8,512]{2,1,0:T(8,128)S(1)} all-gather(f32[2,8,512]{2,1,0:T(8,128)S(1)} %pad_maximum_fusion.1), channel_id=2, replica_groups=mesh['out_hi'=8,'out_mid'=2,'out_lo'=2,'row'=8,'core'=2,'occ'=2] {'out_h..., dimensions={0}, use_global_device_ids=true | all-gather | bytes 557056 | tf_op jit(solution)/shard_map/all_gather | solution.py:212
  81.0 0.0 all-to-all-done.1
  81.0 1.3 %shard_map.47 = f32[16,16,128]{2,1,0:T(8,128)} custom-call(f32[32,8,512]{2,1,0:T(8,128)S(1)} %all-gather.fitted_ref, f32[1024,256]{1,0:T(8,128)S(1)} %bitcast.22), custom_call_target="tpu_custom_call" | custom-call | tf_op jit(solution)/shard_map/pallas_call | solution.py:140
  82.3 0.0 copy-start.1
  82.3 7.7 %all-to-all-start.2 = ((f32[16,16,128]{2,1,0:T(8,128)}), f32[16,16,128]{2,1,0:T(8,128)S(1)}, u32[]{:S(2)}, u32[]{:S(2)}) async-start(f32[16,16,128]{2,1,0:T(8,128)} %shard_map.47), calls=%async_computation.2 | async-start | bytes 262144 | tf_op jit(solution)/shard_map/all_to_all | solution.py:228
  90.0 0.0 copy-done.1
  90.0 0.1 copy.8
  90.2 0.1 broadcast_multiply_fusion.1
  90.3 0.2 mul.62
  90.5 0.4 mul.63
  90.9 0.2 mul.64
  91.1 0.2 mul.65
  91.3 0.1 broadcast_multiply_fusion.blocks_ref
  91.3 0.1 shard_map.48.blocks_ref
  91.5 6.3 %all-to-all-done.2 = f32[16,16,128]{2,1,0:T(8,128)S(1)} async-done(((f32[16,16,128]{2,1,0:T(8,128)}), f32[16,16,128]{2,1,0:T(8,128)S(1)}, u32[]{:S(2)}, u32[]{:S(2)}) %all-to-all-start.2) | async-done | bytes 131104 | tf_op jit(solution)/shard_map/all_to_all | solution.py:228
  97.8 1.3 %shard_map.49 = f32[16,32,64]{2,1,0:T(8,128)} custom-call(f32[2,128,128]{2,1,0:T(8,128)S(1)} %bitcast.23, bf16[3,2,128,512]{3,2,1,0:T(8,128)(2,1)S(1)} %shard_map.48.blocks_ref), custom_call_target="tpu_custom_call" | custom-call | tf_op jit(solution)/shard_map/pallas_call | solution.py:183
  (13 shorter events, 0.2 us)
Async XLA Ops:
  0.0 0.8 copy-start
  1.1 23.0 %collective-permute-start.1 = (f32[64,256]{1,0:T(8,128)S(1)}, f32[64,256]{1,0:T(8,128)S(1)}, u32[]{:S(2)}, u32[]{:S(2)}) collective-permute-start(f32[64,256]{1,0:T(8,128)S(1)} %convolution_bitcast_fusion), channel_id=1, source_target_pairs={{0,32},{32,0},{1,33},{33,1},{2,34},{34,2},{3,35},{35,3},{4,36},{36... | collective-permute-start | bytes 196616 | tf_op jit(solution)/shard_map/ppermute | solution.py:218
  8.8 25.7 %all-to-all-start = ((f32[32,8,512]{2,1,0:T(8,128)}), f32[32,8,512]{2,1,0:T(8,128)S(1)}, u32[]{:S(2)}, u32[]{:S(2)}) async-start(f32[32,8,512]{2,1,0:T(8,128)} %bitcast.24), calls=%async_computation | async-start | bytes 1048576 | tf_op jit(solution)/shard_map/all_to_all | solution.py:208
  35.6 45.4 %all-to-all-start.1 = ((f32[16,64,256]{2,1,0:T(8,128)}), f32[16,64,256]{2,1,0:T(8,128)S(1)}, u32[]{:S(2)}, u32[]{:S(2)}) async-start(f32[16,64,256]{2,1,0:T(8,128)} %bitcast.8), calls=%async_computation.1 | async-start | bytes 2097152 | tf_op jit(solution)/shard_map/all_to_all | solution.py:225
  40.9 5.7 %collective-permute-start = (f32[8,512]{1,0:T(8,128)S(1)}, f32[8,512]{1,0:T(8,128)S(1)}, u32[]{:S(2)}, u32[]{:S(2)}) collective-permute-start(f32[8,512]{1,0:T(8,128)S(1)} %reduce_sum.9), channel_id=1, source_target_pairs={{0,64},{64,0},{1,65},{65,1},{2,66},{66,2},{3,67},{67,3},{4,68},{68... | collective-permute-start | bytes 49160 | tf_op jit(solution)/shard_map/ppermute | solution.py:210
  82.3 7.7 %copy-start.1 = (f32[64,64]{1,0:T(8,128)S(1)}, f32[64,64]{1,0:T(8,128)}, u32[]{:S(2)}) copy-start(f32[64,64]{1,0:T(8,128)} %hole_ref.1) | copy-start | bytes 49156
  82.3 15.5 %all-to-all-start.2 = ((f32[16,16,128]{2,1,0:T(8,128)}), f32[16,16,128]{2,1,0:T(8,128)S(1)}, u32[]{:S(2)}, u32[]{:S(2)}) async-start(f32[16,16,128]{2,1,0:T(8,128)} %shard_map.47), calls=%async_computation.2 | async-start | bytes 262144 | tf_op jit(solution)/shard_map/all_to_all | solution.py:228

commit v8 on v7

--- a/solution.py
+++ b/solution.py
@@ -11,6 +11,7 @@
 pair = ("out_lo", "row")
 lanes = 128
 room = 16 * 1024 * 1024
+steps_out = 4
 
 
 def dot(a, b):
@@ -161,7 +162,7 @@
     )(blocks)
 
 
-def finish_kernel(ladder_ref, blocks_ref, out_ref, held):
+def finish_kernel(ladder_ref, blocks_ref, out_ref, held, result, left):
     lots = blocks_ref.shape[1]
     total = None
     for z in range(lots):
@@ -172,10 +173,17 @@
     lines = out_ref.shape[1] // kinds
     for s in range(kinds):
         held[s] = total[:, s * lanes : (s + 1) * lanes]
-    for s in range(kinds):
-        for r in range(rows):
-            line = held[s, pl.ds(r, lines, stride=rows), :]
-            out_ref[r, pl.ds(s, lines, stride=kinds), :] = line[:, :norbs]
+    lot, sends = rows // steps_out, []
+    for q in range(steps_out):
+        for r in range(q * lot, (q + 1) * lot):
+            for s in range(kinds):
+                line = held[s, pl.ds(r, lines, stride=rows), :]
+                result[r, pl.ds(s, lines, stride=kinds), :] = line[:, :norbs]
+        part = pl.ds(q * lot, lot)
+        sends.append(pltpu.make_async_copy(result.at[part], out_ref.at[part], left.at[q]))
+        sends[-1].start()
+    for send in sends:
+        send.wait()
 
 
 def finish(ladder, blocks, shape):
@@ -184,8 +192,12 @@
         finish_kernel,
         out_shape=jax.ShapeDtypeStruct(shape, jnp.float32),
         in_specs=[pl.BlockSpec(memory_space=pltpu.VMEM)] * 2,
-        out_specs=pl.BlockSpec(memory_space=pltpu.VMEM),
-        scratch_shapes=[pltpu.VMEM((kinds, ladder.shape[1], lanes), jnp.float32)],
+        out_specs=pl.BlockSpec(memory_space=pl.ANY),
+        scratch_shapes=[
+            pltpu.VMEM((kinds, ladder.shape[1], lanes), jnp.float32),
+            pltpu.VMEM(shape, jnp.float32),
+            pltpu.SemaphoreType.DMA((steps_out,)),
+        ],
         compiler_params=pltpu.CompilerParams(vmem_limit_bytes=room),
     )(ladder, blocks)
 

time: 99.7 us -> 99.7 us (level)
  no operation moved by 1% of the time
where the time goes in v8:
time: 99.7 us; the launch traced here: 99.1 us
  starting transfers between devices  34.4 us (35%)
  blocking collectives  34.4 us (35%)
  waiting for transfers between devices  20.4 us (20%)
  Pallas kernels  6.2 us (6%)
  local copies, waits for them, and re-layouts  2.98 us (3%)
    all_gather x1, blocking collectives, local(): whole = lax.all_gather(both, ('out_hi', 'core'), axis=0)  34.4 us
    all_to_all x1, starting transfers between devices, local(): parts = lax.all_to_all(share, plane, 0, 0, tiled=True)  15.2 us
    all_to_all x1, waiting for transfers between devices, local(): parts = lax.all_to_all(share, plane, 0, 0, tiled=True)  10.4 us
    all_to_all x1, starting transfers between devices, local(): ladder = lax.all_to_all(ladder, pair, 0, 0, tiled=True)  7.69 us
    all_to_all x1, waiting for transfers between devices, local(): ladder = lax.all_to_all(ladder, pair, 0, 0, tiled=True)  6.3 us
    all_to_all x1, starting transfers between devices, local(): lax.all_to_all(factors.reshape(cons, *factors.shape[2:]), con, 0, 0, tile...  5.22 us
    ppermute x1, starting transfers between devices, local(): other = lax.ppermute(mine, 'out_lo', [(0, 1), (1, 0)])  4.36 us
    ppermute x1, waiting for transfers between devices, local(): beyond = lax.ppermute(fitted, 'out_mid', [(0, 1), (1, 0)])  3.74 us
  transfers between devices with their start and end apart: 5, of which 3 were waited for; matrix products, arithmetic and copies ran while one was open for 1% of the time, Pallas kernels for 4%

profile of v8, /device:TPU:1, one launch (start us, length us, event | category | flops | bytes accessed | tf_op | source)
XLA Modules:
  0.0 99.1 jit_solution(13665353447483684709)
XLA Ops:
  0.0 0.0 copy-start
  0.0 0.8 copy-done
  0.8 0.2 convolution_bitcast_fusion
  1.1 4.4 %collective-permute-start.1 = (f32[64,256]{1,0:T(8,128)S(1)}, f32[64,256]{1,0:T(8,128)S(1)}, u32[]{:S(2)}, u32[]{:S(2)}) collective-permute-start(f32[64,256]{1,0:T(8,128)S(1)} %convolution_bitcast_fusion), channel_id=1, source_target_pairs={{0,32},{32,0},{1,33},{33,1},{2,34},{34,2},{3,35},{35,3},{4,36},{36... | collective-permute-start | bytes 196616 | tf_op jit(solution)/shard_map/ppermute | solution.py:230
  5.4 3.4 %shard_map.46 = f32[16,2,8,512]{3,2,1,0:T(8,128)} custom-call(f32[32,2,128]{2,1,0:T(2,128)} %bitcast.27, f32[2,4,128,128]{3,2,1,0:T(8,128)} %bitcast.25, f32[64,64]{1,0:T(8,128)} %hole_ref.1), custom_call_target="tpu_custom_call" | custom-call | tf_op jit(solution)/shard_map/pallas_call | solution.py:105
  8.8 15.2 %all-to-all-start = ((f32[32,8,512]{2,1,0:T(8,128)}), f32[32,8,512]{2,1,0:T(8,128)S(1)}, u32[]{:S(2)}, u32[]{:S(2)}) async-start(f32[32,8,512]{2,1,0:T(8,128)} %bitcast.24), calls=%async_computation | async-start | bytes 1048576 | tf_op jit(solution)/shard_map/all_to_all | solution.py:220
  24.1 0.0 collective-permute-done.1
  24.2 10.4 %all-to-all-done = f32[32,8,512]{2,1,0:T(8,128)S(1)} async-done(((f32[32,8,512]{2,1,0:T(8,128)}), f32[32,8,512]{2,1,0:T(8,128)S(1)}, u32[]{:S(2)}, u32[]{:S(2)}) %all-to-all-start) | async-done | bytes 524320 | tf_op jit(solution)/shard_map/all_to_all | solution.py:220
  34.5 1.1 %broadcast_in_dim.2 = f32[8,2,64,256]{3,2,1,0:T(8,128)} broadcast(f32[2,64,256]{2,1,0:T(8,128)S(1)} %pad_maximum_fusion), dimensions={1,2,3} | broadcast | bytes 1179648 | tf_op jit(solution)/shard_map/broadcast_in_dim | solution.py:236
  35.6 5.2 %all-to-all-start.1 = ((f32[16,64,256]{2,1,0:T(8,128)}), f32[16,64,256]{2,1,0:T(8,128)S(1)}, u32[]{:S(2)}, u32[]{:S(2)}) async-start(f32[16,64,256]{2,1,0:T(8,128)} %bitcast.8), calls=%async_computation.1 | async-start | bytes 2097152 | tf_op jit(solution)/shard_map/all_to_all | solution.py:237
  40.9 1.9 %collective-permute-start = (f32[8,512]{1,0:T(8,128)S(1)}, f32[8,512]{1,0:T(8,128)S(1)}, u32[]{:S(2)}, u32[]{:S(2)}) collective-permute-start(f32[8,512]{1,0:T(8,128)S(1)} %reduce_sum.9), channel_id=1, source_target_pairs={{0,64},{64,0},{1,65},{65,1},{2,66},{66,2},{3,67},{67,3},{4,68},{68... | collective-permute-start | bytes 49160 | tf_op jit(solution)/shard_map/ppermute | solution.py:222
  42.8 3.7 %collective-permute-done = f32[8,512]{1,0:T(8,128)S(1)} collective-permute-done((f32[8,512]{1,0:T(8,128)S(1)}, f32[8,512]{1,0:T(8,128)S(1)}, u32[]{:S(2)}, u32[]{:S(2)}) %collective-permute-start) | collective-permute-done | bytes 16416 | tf_op jit(solution)/shard_map/ppermute | solution.py:222
  46.6 34.4 %all-gather.fitted_ref = f32[32,8,512]{2,1,0:T(8,128)S(1)} all-gather(f32[2,8,512]{2,1,0:T(8,128)S(1)} %pad_maximum_fusion.1), channel_id=2, replica_groups=mesh['out_hi'=8,'out_mid'=2,'out_lo'=2,'row'=8,'core'=2,'occ'=2] {'out_h..., dimensions={0}, use_global_device_ids=true | all-gather | bytes 557056 | tf_op jit(solution)/shard_map/all_gather | solution.py:224
  81.0 0.0 all-to-all-done.1
  81.0 1.3 %shard_map.47 = f32[16,16,128]{2,1,0:T(8,128)} custom-call(f32[32,8,512]{2,1,0:T(8,128)S(1)} %all-gather.fitted_ref, f32[1024,256]{1,0:T(8,128)S(1)} %bitcast.22), custom_call_target="tpu_custom_call" | custom-call | tf_op jit(solution)/shard_map/pallas_call | solution.py:141
  82.3 0.0 copy-start.1
  82.3 7.7 %all-to-all-start.2 = ((f32[16,16,128]{2,1,0:T(8,128)}), f32[16,16,128]{2,1,0:T(8,128)S(1)}, u32[]{:S(2)}, u32[]{:S(2)}) async-start(f32[16,16,128]{2,1,0:T(8,128)} %shard_map.47), calls=%async_computation.2 | async-start | bytes 262144 | tf_op jit(solution)/shard_map/all_to_all | solution.py:240
  90.0 0.0 copy-done.1
  90.0 0.1 copy.8
  90.2 0.1 broadcast_multiply_fusion.1
  90.3 0.2 mul.62
  90.5 0.4 mul.63
  90.9 0.2 mul.64
  91.1 0.2 mul.65
  91.3 0.1 broadcast_multiply_fusion.blocks_ref
  91.3 0.1 shard_map.48.blocks_ref
  91.5 6.3 %all-to-all-done.2 = f32[16,16,128]{2,1,0:T(8,128)S(1)} async-done(((f32[16,16,128]{2,1,0:T(8,128)}), f32[16,16,128]{2,1,0:T(8,128)S(1)}, u32[]{:S(2)}, u32[]{:S(2)}) %all-to-all-start.2) | async-done | bytes 131104 | tf_op jit(solution)/shard_map/all_to_all | solution.py:240
  97.8 1.3 %shard_map.49 = f32[16,32,64]{2,1,0:T(8,128)} custom-call(f32[2,128,128]{2,1,0:T(8,128)S(1)} %bitcast.23, bf16[3,2,128,512]{3,2,1,0:T(8,128)(2,1)S(1)} %shard_map.48.blocks_ref), custom_call_target="tpu_custom_call" | custom-call | tf_op jit(solution)/shard_map/pallas_call | solution.py:191
  (13 shorter events, 0.2 us)
Async XLA Ops:
  0.0 0.8 copy-start
  1.1 23.0 %collective-permute-start.1 = (f32[64,256]{1,0:T(8,128)S(1)}, f32[64,256]{1,0:T(8,128)S(1)}, u32[]{:S(2)}, u32[]{:S(2)}) collective-permute-start(f32[64,256]{1,0:T(8,128)S(1)} %convolution_bitcast_fusion), channel_id=1, source_target_pairs={{0,32},{32,0},{1,33},{33,1},{2,34},{34,2},{3,35},{35,3},{4,36},{36... | collective-permute-start | bytes 196616 | tf_op jit(solution)/shard_map/ppermute | solution.py:230
  8.8 25.7 %all-to-all-start = ((f32[32,8,512]{2,1,0:T(8,128)}), f32[32,8,512]{2,1,0:T(8,128)S(1)}, u32[]{:S(2)}, u32[]{:S(2)}) async-start(f32[32,8,512]{2,1,0:T(8,128)} %bitcast.24), calls=%async_computation | async-start | bytes 1048576 | tf_op jit(solution)/shard_map/all_to_all | solution.py:220
  35.6 45.4 %all-to-all-start.1 = ((f32[16,64,256]{2,1,0:T(8,128)}), f32[16,64,256]{2,1,0:T(8,128)S(1)}, u32[]{:S(2)}, u32[]{:S(2)}) async-start(f32[16,64,256]{2,1,0:T(8,128)} %bitcast.8), calls=%async_computation.1 | async-start | bytes 2097152 | tf_op jit(solution)/shard_map/all_to_all | solution.py:237
  40.9 5.7 %collective-permute-start = (f32[8,512]{1,0:T(8,128)S(1)}, f32[8,512]{1,0:T(8,128)S(1)}, u32[]{:S(2)}, u32[]{:S(2)}) collective-permute-start(f32[8,512]{1,0:T(8,128)S(1)} %reduce_sum.9), channel_id=1, source_target_pairs={{0,64},{64,0},{1,65},{65,1},{2,66},{66,2},{3,67},{67,3},{4,68},{68... | collective-permute-start | bytes 49160 | tf_op jit(solution)/shard_map/ppermute | solution.py:222
  82.3 7.7 %copy-start.1 = (f32[64,64]{1,0:T(8,128)S(1)}, f32[64,64]{1,0:T(8,128)}, u32[]{:S(2)}) copy-start(f32[64,64]{1,0:T(8,128)} %hole_ref.1) | copy-start | bytes 49156
  82.3 15.5 %all-to-all-start.2 = ((f32[16,16,128]{2,1,0:T(8,128)}), f32[16,16,128]{2,1,0:T(8,128)S(1)}, u32[]{:S(2)}, u32[]{:S(2)}) async-start(f32[16,16,128]{2,1,0:T(8,128)} %shard_map.47), calls=%async_computation.2 | async-start | bytes 262144 | tf_op jit(solution)/shard_map/all_to_all | solution.py:240
